TPU v7x, 32 devices: a whole 2x2x4 slice. The times are simulated.
32 devices in a mesh: blk: 8 (over z, x), col: 4 (over y, core).
Axes of the slice: x: 2, y: 2, z: 4, core: 2. Of those that a mesh axis runs over, the one named last changes fastest.
Arguments:
- points: bfloat16 [4096, 128], P(('blk', 'col')), may hold values from -4.5 to 4.5
- targets: float32 [4096, 32], P(('blk', 'col')), may hold values from -6 to 6
- pivots: int32 [2, 256], replicated, may hold values from 0 to 4095, as said below
Outputs:
- factor: bfloat16 [4096, 512], P(('blk', 'col'))
- solution: float32 [4096, 32], P(('blk', 'col'))
- residual: float32 [4096, 32], P(('blk', 'col'))
Inputs may be any that keep to these rules, and one draw needn't show every extreme that they name: `pivots`: the 512 indices are distinct; 0 and 4095 are among them.
All inputs are finite; a program needn't handle non-finite values.
Results may differ from a plain program's by a relative error of at most 0.012.
Values may be sent and summed in bfloat16 or wider, within the bound.
A program may use at most 64 MiB of HBM per device.

v0:
```python
import functools

import jax
import jax.numpy as jnp
from jax import lax
from jax.experimental import pallas as pl
from jax.experimental.pallas import tpu as pltpu
from jax.sharding import PartitionSpec as P

FEATURES = 128
ITERS = 3
LANES = 128


noise_level = 0.5
jitter_level = 0.05
highest = lax.Precision.HIGHEST
MESH = pl.DeviceIdType.MESH


def squared_norms(point_rows):
    wide_rows = point_rows.astype(jnp.float32)
    return jnp.sum(wide_rows * wide_rows, axis=1)


def kernel_block(left_rows, left_norms, right_rows, right_norms):
    inner = lax.dot_general(
        left_rows, right_rows, (((1,), (1,)), ((), ())), preferred_element_type=jnp.float32
    )
    distance = left_norms[:, None] + right_norms[None, :] - 2.0 * inner
    return jnp.exp(-2.0 * distance / FEATURES)


def lower_inverse_rows(rows):
    count = len(rows)
    lane = lax.broadcasted_iota(jnp.int32, (8, LANES), 1)
    sub = lax.broadcasted_iota(jnp.int32, (8, LANES), 0)

    def full_of(values):
        return jnp.broadcast_to(values, (8, LANES))

    rows = list(rows)
    done = []
    for p in range(count):
        base = 8 * p
        inside = (lane >= base) & (lane < base + 8)
        cols = [full_of(rows[p][:, base + c : base + c + 1]) for c in range(8)]
        forward = jnp.where(inside, jnp.where(lane == sub + base, 1.0, 0.0), rows[p])
        pivots = jnp.ones((8, LANES), jnp.float32)
        recips, spread_rows, coefs = [], [], []
        for j in range(8):
            pivot = full_of(cols[j][j : j + 1])
            recip = 1.0 / pivot
            pivots = jnp.where(sub == j, pivot, pivots)
            below = jnp.where(sub > j, cols[j] * recip, 0.0)
            spread_row = full_of(forward[j : j + 1])
            forward = forward - below * spread_row
            coef = {c: full_of(cols[c][j : j + 1]) for c in range(j + 1, 8)}
            for c in range(j + 1, 8):
                cols[c] = cols[c] - below * coef[c]
            recips.append(recip)
            spread_rows.append(spread_row)
            coefs.append(coef)
        done.append(jnp.where(lane <= sub + base, forward, 0.0) * lax.rsqrt(pivots))
        for v in range(p + 1, count):
            own = [full_of(rows[v][:, base + c : base + c + 1]) for c in range(8)]
            new = jnp.where(inside, 0.0, rows[v])
            for j in range(8):
                multiplier = own[j] * recips[j]
                new = new - multiplier * spread_rows[j]
                for c in range(j + 1, 8):
                    own[c] = own[c] - multiplier * coefs[j][c]
            rows[v] = new
    return done


def chol_kernel(matrix_ref, out_ref, work):
    blocks = matrix_ref.shape[0] // LANES
    work[...] = matrix_ref[...]
    row_at = lax.broadcasted_iota(jnp.int32, (LANES, LANES), 0)
    col_at = lax.broadcasted_iota(jnp.int32, (LANES, LANES), 1)
    lane_at = lax.broadcasted_iota(jnp.int32, (LANES, matrix_ref.shape[1]), 1)

    def one_block(j, carry):
        at = pl.multiple_of(j * LANES, LANES)
        here_rows = pl.ds(at, LANES)
        inverse = jnp.concatenate(
            lower_inverse_rows(
                [work[pl.ds(at + 8 * v, 8), pl.ds(at, LANES)] for v in range(LANES // 8)]
            ),
            axis=0,
        )
        work[here_rows, pl.ds(at, LANES)] = jnp.where(row_at == col_at, 1.0, 0.0)
        side = jnp.dot(
            inverse, work[here_rows, :], precision=highest, preferred_element_type=jnp.float32
        )
        out_ref[here_rows, :] = jnp.where(lane_at < at + LANES, side, 0.0)
        work[here_rows, :] = side

        def below(i, inner):
            to = pl.multiple_of(i * LANES, LANES)
            rows = work[pl.ds(to, LANES), :]
            rows = jnp.where((lane_at >= at) & (lane_at < at + LANES), 0.0, rows)
            work[pl.ds(to, LANES), :] = rows - lax.dot_general(
                work[here_rows, pl.ds(to, LANES)],
                side,
                (((0,), (0,)), ((), ())),
                precision=highest,
                preferred_element_type=jnp.float32,
            )
            return inner

        lax.fori_loop(j + 1, blocks, below, 0)
        return carry

    lax.fori_loop(0, blocks, one_block, 0)


def chol_inverse(matrix):
    vmem = pl.BlockSpec(memory_space=pltpu.VMEM)
    return pl.pallas_call(
        chol_kernel,
        out_shape=jax.ShapeDtypeStruct(matrix.shape, jnp.float32),
        in_specs=[vmem],
        out_specs=vmem,
        scratch_shapes=[pltpu.VMEM(matrix.shape, jnp.float32)],
        name="chol_inverse",
    )(matrix)


def build_factor(point_rows, picked):
    picked_norms = squared_norms(picked)
    identity = jnp.eye(picked.shape[0], dtype=jnp.float32)
    inverse = chol_inverse(
        kernel_block(picked, picked_norms, picked, picked_norms) + jitter_level * identity
    )
    cross = kernel_block(point_rows, squared_norms(point_rows), picked, picked_norms)
    return jnp.dot(cross, inverse.T, precision=highest)


def upper_blocks(count):
    return [(j, i) for i in range(count) for j in range(i + 1)]


def pack_upper(matrix):
    count = matrix.shape[0] // LANES
    return jnp.concatenate(
        [
            matrix[i * LANES : (i + 1) * LANES, j * LANES : (j + 1) * LANES]
            for i, j in upper_blocks(count)
        ],
        axis=0,
    )


def unpack_upper(packed, order):
    count = order // LANES
    blocks = {
        at: packed[k * LANES : (k + 1) * LANES] for k, at in enumerate(upper_blocks(count))
    }
    empty = jnp.zeros((LANES, LANES), packed.dtype)
    return jnp.concatenate(
        [
            jnp.concatenate([blocks.get((i, j), empty) for j in range(count)], axis=1)
            for i in range(count)
        ],
        axis=0,
    )


def here(width):
    return lax.axis_index("blk") * width + lax.axis_index("col")


def coords(index, width):
    return (lax.div(index, width), lax.rem(index, width))


def greet(n, width, me):
    barrier = pltpu.get_barrier_semaphore()

    def hello(i, carry):
        peer = lax.rem(me + i, n)
        pl.semaphore_signal(
            barrier, inc=1, device_id=coords(peer, width), device_id_type=MESH
        )
        return carry

    lax.fori_loop(1, n, hello, 0)
    pl.semaphore_wait(barrier, n - 1)


def spread(n, width, me, src, dst, send_sem, recv_sem):
    def push(i, carry):
        peer = lax.rem(me + i, n)
        pltpu.make_async_remote_copy(
            src_ref=src(peer, i),
            dst_ref=dst(peer, i),
            send_sem=send_sem,
            recv_sem=recv_sem,
            device_id=coords(peer, width),
            device_id_type=MESH,
        ).start()
        return carry

    lax.fori_loop(1, n, push, 0)


def drain(ref, sem):
    pltpu.make_async_copy(ref, ref, sem).wait()


def gather_kernel(n, width, own_ref, all_ref, send_sem, recv_sem, own_sem):
    me = here(width)
    keep = pltpu.make_async_copy(own_ref, all_ref.at[me], own_sem)
    keep.start()
    greet(n, width, me)
    spread(
        n, width, me, lambda peer, i: own_ref, lambda peer, i: all_ref.at[me], send_sem, recv_sem
    )
    drain(all_ref.at[pl.ds(0, n - 1)], recv_sem)
    drain(all_ref.at[pl.ds(0, n - 1)], send_sem)
    keep.wait()


def gather_all(own, n, width):
    vmem = pl.BlockSpec(memory_space=pltpu.VMEM)
    return pl.pallas_call(
        functools.partial(gather_kernel, n, width),
        out_shape=jax.ShapeDtypeStruct((n,) + own.shape, own.dtype),
        in_specs=[vmem],
        out_specs=vmem,
        scratch_shapes=[pltpu.SemaphoreType.DMA] * 3,
        compiler_params=pltpu.CompilerParams(collective_id=0, has_side_effects=True),
        name="gather_points",
    )(own)


def reduce_kernel(n, width, part_ref, out_ref, got_ref, send_sem, recv_sem, send2_sem, recv2_sem):
    me = here(width)
    greet(n, width, me)
    spread(
        n,
        width,
        me,
        lambda peer, i: part_ref.at[peer],
        lambda peer, i: got_ref.at[i - 1],
        send_sem,
        recv_sem,
    )
    drain(got_ref, recv_sem)
    total = lax.fori_loop(0, n - 1, lambda i, acc: acc + got_ref[i], part_ref[me])
    out_ref[me] = total
    spread(
        n,
        width,
        me,
        lambda peer, i: out_ref.at[me],
        lambda peer, i: out_ref.at[me],
        send2_sem,
        recv2_sem,
    )
    drain(got_ref, send_sem)
    drain(got_ref, recv2_sem)
    drain(got_ref, send2_sem)


def reduce_all(part, n, width):
    vmem = pl.BlockSpec(memory_space=pltpu.VMEM)
    pieces = part.reshape(n, part.shape[0] // n, part.shape[1])
    summed = pl.pallas_call(
        functools.partial(reduce_kernel, n, width),
        out_shape=jax.ShapeDtypeStruct(pieces.shape, pieces.dtype),
        in_specs=[vmem],
        out_specs=vmem,
        scratch_shapes=[pltpu.VMEM((n - 1,) + pieces.shape[1:], pieces.dtype)]
        + [pltpu.SemaphoreType.DMA] * 4,
        compiler_params=pltpu.CompilerParams(collective_id=1, has_side_effects=True),
        name="sum_gram",
    )(pieces)
    return summed.reshape(part.shape)


def cg_kernel(
    n,
    width,
    owners,
    tile_ref,
    rhs_ref,
    wide_ref,
    inverse_ref,
    sol_ref,
    res_ref,
    dirs,
    put,
    got,
    ans,
    kept_proj,
    kept_squares,
    kept_rz,
    dir_send,
    dir_recv,
    put_send,
    put_recv,
    ans_send,
    ans_recv,
):
    me = here(width)
    rhs_count, row_count = rhs_ref.shape
    per = rhs_count // owners
    order = wide_ref.shape[1]
    lanes = order // LANES
    all_own = owners == n
    greet(n, width, me)

    def only_owners(body):
        if all_own:
            body()
        else:
            pl.when(me < owners)(body)

    def wide_sum(values):
        return jnp.broadcast_to(jnp.sum(values, axis=1, keepdims=True), (values.shape[0], LANES))

    def to_owners(k, proj, sums):
        for q in range(lanes):
            put[k, :, q, :] = proj[:, q * LANES : (q + 1) * LANES]
        for s, value in enumerate(sums):
            put[k, :, lanes + s, :] = value

        def push(i, carry):
            peer = lax.rem(me + i, owners)

            def go():
                pltpu.make_async_remote_copy(
                    src_ref=put.at[k, pl.ds(peer * per, per)],
                    dst_ref=got.at[k, lax.rem(me - peer + n, n) - 1],
                    send_sem=put_send.at[k],
                    recv_sem=put_recv.at[k],
                    device_id=coords(peer, width),
                    device_id_type=MESH,
                ).start()

            if all_own:
                go()
            else:
                pl.when(peer != me)(go)
            return carry

        lax.fori_loop(1 if all_own else 0, owners, push, 0)

    def finish_put(k):
        if all_own:
            drain(put.at[k, pl.ds(0, (owners - 1) * per)], put_send.at[k])
        else:

            @pl.when(me < owners)
            def _():
                drain(put.at[k, pl.ds(0, (owners - 1) * per)], put_send.at[k])

            @pl.when(me >= owners)
            def _():
                drain(put.at[k], put_send.at[k])

    def collect(k):
        drain(got.at[k], put_recv.at[k])
        start = put[k, pl.ds(me * per, per)]
        return lax.fori_loop(0, n - 1, lambda i, acc: acc + got[k, i], start)

    def answer(k, rows):
        for s, value in enumerate(rows):
            ans[k, pl.ds(me * per, per), s, :] = value
        spread(
            n,
            width,
            me,
            lambda peer, i: ans.at[k, pl.ds(me * per, per)],
            lambda peer, i: ans.at[k, pl.ds(me * per, per)],
            ans_send.at[k],
            ans_recv.at[k],
        )

    def await_answer(k):
        if all_own:
            drain(ans.at[k, pl.ds(0, (owners - 1) * per)], ans_recv.at[k])
        else:

            @pl.when(me < owners)
            def _():
                drain(ans.at[k, pl.ds(0, (owners - 1) * per)], ans_recv.at[k])

            @pl.when(me >= owners)
            def _():
                drain(ans.at[k], ans_recv.at[k])

    def finish_answer(k):
        def body():
            def one(i, carry):
                drain(ans.at[k, pl.ds(0, per)], ans_send.at[k])
                return carry

            lax.fori_loop(1, n, one, 0)

        only_owners(body)

    def solve(proj):
        half = lax.dot_general(
            proj,
            inverse_ref[...],
            (((1,), (1,)), ((), ())),
            precision=highest,
            preferred_element_type=jnp.float32,
        )
        coef = jnp.dot(
            half, inverse_ref[...], precision=highest, preferred_element_type=jnp.float32
        )
        return coef, wide_sum(half * half)

    def split(row):
        return [row[:, q * LANES : (q + 1) * LANES] for q in range(lanes)]

    def project(rows):
        return jnp.dot(rows, wide_ref[...], precision=highest, preferred_element_type=jnp.float32)

    def joined(packed):
        return jnp.concatenate([packed[:, q, :] for q in range(lanes)], axis=1)

    def precondition(residual, k):
        packed = ans[k]
        back = lax.dot_general(
            joined(packed),
            wide_ref[...],
            (((1,), (1,)), ((), ())),
            precision=highest,
            preferred_element_type=jnp.float32,
        )
        return (residual - back) * (1.0 / noise_level)

    residual = rhs_ref[...]
    solution = jnp.zeros_like(residual)
    to_owners(0, project(residual), [wide_sum(residual * residual)])

    def first_answer():
        total = collect(0)
        proj = joined(total)
        squares = total[:, lanes, :]
        coef, covered = solve(proj)
        kept_proj[...] = proj
        kept_squares[...] = squares
        kept_rz[...] = (squares - covered) * (1.0 / noise_level)
        answer(0, split(coef))

    def later_answer(k, last):
        total = collect(k)
        rz_before = kept_rz[...]
        size = rz_before / total[:, lanes, :]
        if last:
            answer(k, [size] * (lanes + 2))
            return
        along, image_squares = total[:, lanes + 1, :], total[:, lanes + 2, :]
        size_row = jnp.concatenate([size] * lanes, axis=1)
        proj = kept_proj[...] - size_row * joined(total)
        squares = kept_squares[...] - 2.0 * size * along + size * size * image_squares
        coef, covered = solve(proj)
        rz = (squares - covered) * (1.0 / noise_level)
        kept_proj[...] = proj
        kept_squares[...] = squares
        kept_rz[...] = rz
        answer(k, split(coef) + [size, rz / rz_before])

    only_owners(first_answer)
    await_answer(0)
    direction = precondition(residual, 0)

    for step_index in range(ITERS):
        last = step_index + 1 == ITERS
        dirs[step_index, me] = direction
        spread(
            n,
            width,
            me,
            lambda peer, i: dirs.at[step_index, me],
            lambda peer, i: dirs.at[step_index, me],
            dir_send.at[step_index],
            dir_recv.at[step_index],
        )
        drain(dirs.at[step_index, pl.ds(0, n - 1)], dir_recv.at[step_index])

        def multiply(j, acc):
            return acc + jnp.dot(
                dirs[step_index, j],
                tile_ref[j],
                precision=highest,
                preferred_element_type=jnp.float32,
            )

        image = lax.fori_loop(0, n, multiply, noise_level * direction, unroll=4)
        k = step_index + 1
        sums = [wide_sum(direction * image)]
        if last:
            to_owners(k, jnp.zeros((rhs_count, order), jnp.float32), sums)
        else:
            to_owners(
                k, project(image), sums + [wide_sum(residual * image), wide_sum(image * image)]
            )
        only_owners(functools.partial(later_answer, k, last))
        await_answer(k)
        size = ans[k, :, lanes, :]
        solution = solution + size * direction
        residual = residual - size * image
        if not last:
            direction = precondition(residual, k) + ans[k, :, lanes + 1, :] * direction
    sol_ref[...] = solution
    res_ref[...] = residual
    for step_index in range(ITERS):
        drain(dirs.at[step_index, pl.ds(0, n - 1)], dir_send.at[step_index])
    for k in range(ITERS + 1):
        finish_put(k)
        finish_answer(k)


def solve_cg(tile, targets_t, wide_factor, inverse, n, width):
    rhs_count, row_count = targets_t.shape
    owners = min(n, rhs_count)
    per = rhs_count // owners
    order = wide_factor.shape[1]
    rows = -(-(order // LANES + 3) // 8) * 8
    vmem = pl.BlockSpec(memory_space=pltpu.VMEM)
    f32 = jnp.float32
    return pl.pallas_call(
        functools.partial(cg_kernel, n, width, owners),
        out_shape=[jax.ShapeDtypeStruct((rhs_count, row_count), f32)] * 2,
        in_specs=[vmem] * 4,
        out_specs=[vmem] * 2,
        scratch_shapes=[
            pltpu.VMEM((ITERS, n, rhs_count, row_count), f32),
            pltpu.VMEM((ITERS + 1, rhs_count, rows, LANES), f32),
            pltpu.VMEM((ITERS + 1, n - 1, per, rows, LANES), f32),
            pltpu.VMEM((ITERS + 1, rhs_count, rows, LANES), f32),
            pltpu.VMEM((per, order), f32),
            pltpu.VMEM((per, LANES), f32),
            pltpu.VMEM((per, LANES), f32),
            pltpu.SemaphoreType.DMA((ITERS,)),
            pltpu.SemaphoreType.DMA((ITERS,)),
        ]
        + [pltpu.SemaphoreType.DMA((ITERS + 1,))] * 4,
        compiler_params=pltpu.CompilerParams(collective_id=2, has_side_effects=True),
        name="conjugate_gradients",
    )(tile.reshape(n, row_count, row_count), targets_t, wide_factor, inverse)


def per_device(n, width, points, targets, pivots):
    piv_count = pivots.shape[1]
    all_points = gather_all(points, n, width)
    all_points = all_points.reshape(-1, points.shape[1])
    picked = all_points[pivots.reshape(-1)]
    wide_factor = build_factor(points, picked)
    factor = wide_factor.astype(jnp.bfloat16)
    local_gram = lax.dot_general(
        wide_factor, wide_factor, (((0,), (0,)), ((), ())), precision=highest
    )
    order = 2 * piv_count
    gram = unpack_upper(reduce_all(pack_upper(local_gram), n, width), order)
    inverse = chol_inverse(gram + noise_level * jnp.eye(order, dtype=jnp.float32))
    tile = kernel_block(all_points, squared_norms(all_points), points, squared_norms(points))
    solution_t, residual_t = solve_cg(tile, targets.T, wide_factor, inverse, n, width)
    return (factor, solution_t.T, residual_t.T)


def solution(mesh):
    n, width = mesh.size, mesh.shape["col"]
    return jax.shard_map(
        functools.partial(per_device, n, width),
        mesh=mesh,
        in_specs=(P(("blk", "col"), None), P(("blk", "col"), None), P()),
        out_specs=(P(("blk", "col"), None), P(("blk", "col"), None), P(("blk", "col"), None)),
        check_vma=False,
    )
```

profile of v0, /device:TPU:0, one launch (start us, length us, event | category | flops | bytes accessed | tf_op | source)
XLA Modules:
  0.0 241.8 jit_solution(8454488010436989498)
XLA Ops:
  0.6 0.0 copy-start.2
  0.6 0.9 multiply_reduce_fusion.2
  1.6 0.7 copy.6
  2.3 26.2 %gather_points.1 = bf16[32,128,128]{2,1,0:T(8,128)(2,1)} custom-call(bf16[128,128]{1,0:T(8,128)(2,1)} %own_ref.1), custom_call_target="tpu_custom_call" | custom-call | tf_op jit(solution)/shard_map/gather_points/pallas_call | solution.py:228
  28.5 1.8 multiply_reduce_fusion
  30.3 2.4 gather_fusion
  32.7 0.1 multiply_reduce_fusion.1
  32.9 0.0 copy-done.2
  32.9 0.2 fusion.10
  33.1 1.4 fusion.6.matrix_ref
  34.6 0.0 copy-start
  34.6 22.4 %chol_inverse.2 = f32[512,512]{1,0:T(8,128)} custom-call(f32[512,512]{1,0:T(8,128)} %fusion.6.matrix_ref), custom_call_target="tpu_custom_call" | custom-call | tf_op jit(solution)/shard_map/chol_inverse/pallas_call | solution.py:121
  56.9 3.0 %fusion.13 = (bf16[128,512]{1,0:T(8,128)(2,1)}, f32[128,512]{1,0:T(8,128)S(1)}) fusion(f32[128,512]{1,0:T(8,128)S(1)} %fusion.10, f32[512,512]{1,0:T(8,128)} %chol_inverse.2), kind=kOutput, calls=%fused_computation.26 | convolution fusion | flops 402718720 | bytes 1703936 | tf_op jit(solution)/shard_map/dot_general | solution.py:138
  60.0 0.0 copy-start.1
  60.0 0.0 copy-done
  60.0 1.9 fusion.2
  61.8 1.0 fusion.14
  62.9 0.0 copy-done.1
  63.0 0.9 pad_maximum_fusion
  63.9 35.8 %sum_gram.1 = f32[32,40,128]{2,1,0:T(8,128)} custom-call(f32[32,40,128]{2,1,0:T(8,128)} %bitcast.34), custom_call_target="tpu_custom_call" | custom-call | tf_op jit(solution)/shard_map/sum_gram/pallas_call | solution.py:271
  99.7 1.2 fusion.12
  100.9 1.1 fusion.11.matrix_ref
  102.0 22.3 %chol_inverse.3.inverse_ref = f32[512,512]{1,0:T(8,128)} custom-call(f32[512,512]{1,0:T(8,128)} %fusion.11.matrix_ref), custom_call_target="tpu_custom_call" | custom-call | tf_op jit(solution)/shard_map/chol_inverse/pallas_call | solution.py:121
  124.3 114.9 %conjugate_gradients.1 = (f32[32,128]{1,0:T(8,128)}, f32[32,128]{1,0:T(8,128)}) custom-call(f32[32,128,128]{2,1,0:T(8,128)} %bitcast.35, f32[32,128]{1,0:T(8,128)} %bitcast.36, f32[128,512]{1,0:T(8,128)} %copy-done.1, f32[512,512]{1,0:T(8,128)} %chol_inverse.3.inverse_ref), custom_call_target="tpu_custom_call" | custom-call | tf_op jit(solution)/shard_map/conjugate_gradients/pallas_call | solution.py:530
  239.2 1.3 copy.9
  240.5 1.3 copy.10
  (8 shorter events, 0.1 us)
Async XLA Ops:
  0.6 32.3 %copy-start.2 = (bf16[128,128]{1,0:T(8,128)(2,1)S(1)}, bf16[128,128]{1,0:T(8,128)(2,1)}, u32[]{:S(2)}) copy-start(bf16[128,128]{1,0:T(8,128)(2,1)} %own_ref.1) | copy-start | bytes 98308
  34.6 25.4 %copy-start = (bf16[32,128,128]{2,1,0:T(8,128)(2,1)S(1)}, bf16[32,128,128]{2,1,0:T(8,128)(2,1)}, u32[]{:S(2)}) copy-start(bf16[32,128,128]{2,1,0:T(8,128)(2,1)} %gather_points.1) | copy-start | bytes 3145732
  60.0 2.9 %copy-start.1 = (f32[128,512]{1,0:T(8,128)}, f32[128,512]{1,0:T(8,128)S(1)}, u32[]{:S(2)}) copy-start(f32[128,512]{1,0:T(8,128)S(1)} %get-tuple-element.18.wide_ref) | copy-start | bytes 786436
where the time goes:
time: 242 us
  Pallas kernels  222 us (92%)
  matrix products  7.56 us (3%)
  local copies, waits for them, and re-layouts  7.04 us (3%)
  other arithmetic  4.87 us (2%)
    pallas_call x1, Pallas kernels, solve_cg(): pl.pallas_call(functools.partial(cg_kernel, n, width, owners), out_shape=...  115 us
    pallas_call x2, Pallas kernels, chol_inverse(): pl.pallas_call(chol_kernel, out_shape=jax.ShapeDtypeStruct(matrix.shape,...  44.6 us
    pallas_call x1, Pallas kernels, reduce_all(): pl.pallas_call(functools.partial(reduce_kernel, n, width), out_shape=jax....  35.8 us
    pallas_call x1, Pallas kernels, gather_all(): pl.pallas_call(functools.partial(gather_kernel, n, width), out_shape=jax....  26.2 us

commit v1 on v0

--- a/solution.py
+++ b/solution.py
@@ -18,16 +18,31 @@
 MESH = pl.DeviceIdType.MESH
 
 
-def squared_norms(point_rows):
+def dot_t(left, right):
+    return lax.dot_general(
+        left,
+        right,
+        (((1,), (1,)), ((), ())),
+        precision=highest,
+        preferred_element_type=jnp.float32,
+    )
+
+
+def column_norms(point_rows):
     wide_rows = point_rows.astype(jnp.float32)
-    return jnp.sum(wide_rows * wide_rows, axis=1)
+    return jnp.sum(wide_rows * wide_rows, axis=1, keepdims=True)
+
+
+def row_norms(point_rows):
+    wide_rows = point_rows.astype(jnp.float32)
+    return dot_t(jnp.ones((8, wide_rows.shape[1]), jnp.float32), wide_rows * wide_rows)[0:1]
 
 
 def kernel_block(left_rows, left_norms, right_rows, right_norms):
     inner = lax.dot_general(
         left_rows, right_rows, (((1,), (1,)), ((), ())), preferred_element_type=jnp.float32
     )
-    distance = left_norms[:, None] + right_norms[None, :] - 2.0 * inner
+    distance = left_norms + right_norms - 2.0 * inner
     return jnp.exp(-2.0 * distance / FEATURES)
 
 
@@ -74,12 +89,12 @@
     return done
 
 
-def chol_kernel(matrix_ref, out_ref, work):
-    blocks = matrix_ref.shape[0] // LANES
-    work[...] = matrix_ref[...]
+def invert_lower(work, out_ref):
+    order = work.shape[0]
+    blocks = order // LANES
     row_at = lax.broadcasted_iota(jnp.int32, (LANES, LANES), 0)
     col_at = lax.broadcasted_iota(jnp.int32, (LANES, LANES), 1)
-    lane_at = lax.broadcasted_iota(jnp.int32, (LANES, matrix_ref.shape[1]), 1)
+    lane_at = lax.broadcasted_iota(jnp.int32, (LANES, order), 1)
 
     def one_block(j, carry):
         at = pl.multiple_of(j * LANES, LANES)
@@ -116,56 +131,35 @@
     lax.fori_loop(0, blocks, one_block, 0)
 
 
-def chol_inverse(matrix):
+def shifted(matrix, level):
+    row_at = lax.broadcasted_iota(jnp.int32, matrix.shape, 0)
+    col_at = lax.broadcasted_iota(jnp.int32, matrix.shape, 1)
+    return matrix + jnp.where(row_at == col_at, level, 0.0)
+
+
+def pivot_kernel(picked_ref, out_ref, work):
+    picked = picked_ref[...]
+    work[...] = shifted(
+        kernel_block(picked, column_norms(picked), picked, row_norms(picked)), jitter_level
+    )
+    invert_lower(work, out_ref)
+
+
+def gram_kernel(gram_ref, out_ref, work):
+    work[...] = shifted(gram_ref[...], noise_level)
+    invert_lower(work, out_ref)
+
+
+def chol_inverse(kernel, operand, order, name):
     vmem = pl.BlockSpec(memory_space=pltpu.VMEM)
     return pl.pallas_call(
-        chol_kernel,
-        out_shape=jax.ShapeDtypeStruct(matrix.shape, jnp.float32),
+        kernel,
+        out_shape=jax.ShapeDtypeStruct((order, order), jnp.float32),
         in_specs=[vmem],
         out_specs=vmem,
-        scratch_shapes=[pltpu.VMEM(matrix.shape, jnp.float32)],
-        name="chol_inverse",
-    )(matrix)
-
-
-def build_factor(point_rows, picked):
-    picked_norms = squared_norms(picked)
-    identity = jnp.eye(picked.shape[0], dtype=jnp.float32)
-    inverse = chol_inverse(
-        kernel_block(picked, picked_norms, picked, picked_norms) + jitter_level * identity
-    )
-    cross = kernel_block(point_rows, squared_norms(point_rows), picked, picked_norms)
-    return jnp.dot(cross, inverse.T, precision=highest)
-
-
-def upper_blocks(count):
-    return [(j, i) for i in range(count) for j in range(i + 1)]
-
-
-def pack_upper(matrix):
-    count = matrix.shape[0] // LANES
-    return jnp.concatenate(
-        [
-            matrix[i * LANES : (i + 1) * LANES, j * LANES : (j + 1) * LANES]
-            for i, j in upper_blocks(count)
-        ],
-        axis=0,
-    )
-
-
-def unpack_upper(packed, order):
-    count = order // LANES
-    blocks = {
-        at: packed[k * LANES : (k + 1) * LANES] for k, at in enumerate(upper_blocks(count))
-    }
-    empty = jnp.zeros((LANES, LANES), packed.dtype)
-    return jnp.concatenate(
-        [
-            jnp.concatenate([blocks.get((i, j), empty) for j in range(count)], axis=1)
-            for i in range(count)
-        ],
-        axis=0,
-    )
+        scratch_shapes=[pltpu.VMEM((order, order), jnp.float32)],
+        name=name,
+    )(operand)
 
 
 def here(width):
@@ -210,75 +204,290 @@
     pltpu.make_async_copy(ref, ref, sem).wait()
 
 
-def gather_kernel(n, width, own_ref, all_ref, send_sem, recv_sem, own_sem):
+def flip(index, bits):
+    moved = index
+    weight = 1
+    while weight <= bits:
+        if bits & weight:
+            moved = moved + weight * (1 - 2 * lax.rem(lax.div(index, weight), 2))
+        weight *= 2
+    return moved
+
+
+class Relay:
+    def __init__(self, n, width, me, blocks, own, send_sem, recv_sems, pair_sem):
+        self.n, self.width, self.me = n, width, me
+        self.blocks, self.own = blocks, own
+        self.send_sem, self.recv_sems, self.pair_sem = send_sem, recv_sems, pair_sem
+        self.plane = 2 * width
+        self.lines = n // self.plane
+
+    def send(self, src_ref, source, peer, recv_sem):
+        pltpu.make_async_remote_copy(
+            src_ref=src_ref,
+            dst_ref=self.blocks.at[source],
+            send_sem=self.send_sem,
+            recv_sem=recv_sem,
+            device_id=coords(peer, self.width),
+            device_id_type=MESH,
+        ).start()
+
+    def fan(self, src_ref, source, i):
+        for q in range(2, self.plane, 2):
+            sem = self.recv_sems.at[self.lines * (q // 2) + i]
+            self.send(src_ref, source, flip(self.me, q), sem)
+        self.send(src_ref, source, flip(self.me, 1), self.pair_sem)
+
+    def start(self):
+        def along(i, carry):
+            peer = lax.rem(self.me + self.plane * i, self.n)
+            self.send(self.own, self.me, peer, self.recv_sems.at[i])
+            return carry
+
+        lax.fori_loop(1, self.lines, along, 0)
+        self.fan(self.own, self.me, 0)
+
+    def relay_lines(self):
+        def one(i, carry):
+            source = lax.rem(self.me - self.plane * i + self.n, self.n)
+            drain(self.blocks.at[source], self.recv_sems.at[i])
+            self.fan(self.blocks.at[source], source, i)
+            return carry
+
+        lax.fori_loop(1, self.lines, one, 0)
+
+    def relay_plane(self):
+        for q in range(2, self.plane, 2):
+
+            def one(i, carry, q=q):
+                source = lax.rem(flip(self.me, q) - self.plane * i + self.n, self.n)
+                ref = self.blocks.at[source]
+                drain(ref, self.recv_sems.at[self.lines * (q // 2) + i])
+                self.send(ref, source, flip(self.me, 1), self.pair_sem)
+                return carry
+
+            lax.fori_loop(0, self.lines, one, 0)
+
+    def finish(self):
+        drain(self.blocks.at[pl.ds(0, self.n // 2)], self.pair_sem)
+
+    def finish_sends(self):
+        drain(self.blocks.at[pl.ds(0, self.n - 1)], self.send_sem)
+
+
+def gather_kernel(
+    n, width, points_ref, targets_ref, all_points, all_targets, send_sem, recv_sems, pair_sem, own_sem
+):
     me = here(width)
-    keep = pltpu.make_async_copy(own_ref, all_ref.at[me], own_sem)
-    keep.start()
+    keeps = [
+        pltpu.make_async_copy(points_ref, all_points.at[me], own_sem.at[0]),
+        pltpu.make_async_copy(targets_ref, all_targets.at[me], own_sem.at[1]),
+    ]
+    for keep in keeps:
+        keep.start()
     greet(n, width, me)
-    spread(
-        n, width, me, lambda peer, i: own_ref, lambda peer, i: all_ref.at[me], send_sem, recv_sem
-    )
-    drain(all_ref.at[pl.ds(0, n - 1)], recv_sem)
-    drain(all_ref.at[pl.ds(0, n - 1)], send_sem)
-    keep.wait()
-
-
-def gather_all(own, n, width):
+    relays = [
+        Relay(n, width, me, blocks, own, send_sem.at[k], recv_sems.at[k], pair_sem.at[k])
+        for k, (blocks, own) in enumerate([(all_points, points_ref), (all_targets, targets_ref)])
+    ]
+    for relay in relays:
+        relay.start()
+    for relay in relays:
+        relay.relay_lines()
+    for relay in relays:
+        relay.relay_plane()
+    for relay in relays:
+        relay.finish()
+    for relay in relays:
+        relay.finish_sends()
+    for keep in keeps:
+        keep.wait()
+
+
+def gather_all(points, targets_t, n, width):
     vmem = pl.BlockSpec(memory_space=pltpu.VMEM)
     return pl.pallas_call(
         functools.partial(gather_kernel, n, width),
-        out_shape=jax.ShapeDtypeStruct((n,) + own.shape, own.dtype),
-        in_specs=[vmem],
-        out_specs=vmem,
-        scratch_shapes=[pltpu.SemaphoreType.DMA] * 3,
+        out_shape=[jax.ShapeDtypeStruct((n,) + v.shape, v.dtype) for v in (points, targets_t)],
+        in_specs=[vmem] * 2,
+        out_specs=[vmem] * 2,
+        scratch_shapes=[
+            pltpu.SemaphoreType.DMA((2,)),
+            pltpu.SemaphoreType.DMA((2, n // 2)),
+            pltpu.SemaphoreType.DMA((2,)),
+            pltpu.SemaphoreType.DMA((2,)),
+        ],
         compiler_params=pltpu.CompilerParams(collective_id=0, has_side_effects=True),
         name="gather_points",
-    )(own)
-
-
-def reduce_kernel(n, width, part_ref, out_ref, got_ref, send_sem, recv_sem, send2_sem, recv2_sem):
+    )(points, targets_t)
+
+
+def sweep_kernel(
+    n,
+    width,
+    points_ref,
+    targets_ref,
+    picked_ref,
+    inverse_ref,
+    factor_ref,
+    wide_ref,
+    tile_ref,
+    gram_ref,
+    proj_ref,
+    zed_ref,
+    image_ref,
+    square_ref,
+    gram_part,
+    proj_part,
+    zed_part,
+    gram_got,
+    proj_got,
+    zed_got,
+    send_sem,
+    recv_sem,
+):
     me = here(width)
-    greet(n, width, me)
-    spread(
-        n,
-        width,
-        me,
-        lambda peer, i: part_ref.at[peer],
-        lambda peer, i: got_ref.at[i - 1],
-        send_sem,
-        recv_sem,
-    )
-    drain(got_ref, recv_sem)
-    total = lax.fori_loop(0, n - 1, lambda i, acc: acc + got_ref[i], part_ref[me])
-    out_ref[me] = total
-    spread(
-        n,
-        width,
-        me,
-        lambda peer, i: out_ref.at[me],
-        lambda peer, i: out_ref.at[me],
-        send2_sem,
-        recv2_sem,
-    )
-    drain(got_ref, send_sem)
-    drain(got_ref, recv2_sem)
-    drain(got_ref, send2_sem)
-
-
-def reduce_all(part, n, width):
+    core, pair = lax.rem(me, 2), lax.div(me, 2)
+    other = 1 - core
+    partner = flip(me, 1)
+    barrier = pltpu.get_barrier_semaphore()
+    pl.semaphore_signal(barrier, inc=1, device_id=coords(partner, width), device_id_type=MESH)
+    order = inverse_ref.shape[0]
+    half = order // 2
+    chunk = min(4, n // 2)
+    picked = picked_ref[...]
+    picked_column = column_norms(picked)
+    own = points_ref[pair, core]
+    beside = points_ref[pair, other]
+    own_column, beside_column = column_norms(own), column_norms(beside)
+    own_cross = kernel_block(own, own_column, picked, row_norms(picked))
+    wide = jnp.concatenate(
+        [
+            dot_t(own_cross[:, :half], inverse_ref[:half, :half]),
+            dot_t(own_cross, inverse_ref[half:, :]),
+        ],
+        axis=1,
+    )
+    wide_ref[...] = wide
+    factor_ref[...] = wide.astype(jnp.bfloat16)
+    own_targets = targets_ref[pair, core]
+    image_ref[...] = noise_level * own_targets
+    square_ref[...] = jnp.zeros_like(square_ref)
+    zed_ref[...] = noise_level * wide
+    for ref in (gram_part, proj_part, zed_part):
+        ref[...] = jnp.zeros_like(ref)
+
+    def step(i, carry):
+        at = i * chunk
+        near = jnp.concatenate([points_ref[at + t, core] for t in range(chunk)], axis=0)
+        far = jnp.concatenate([points_ref[at + t, other] for t in range(chunk)], axis=0)
+        near_targets = jnp.concatenate([targets_ref[at + t, core] for t in range(chunk)], axis=1)
+        far_targets = jnp.concatenate([targets_ref[at + t, other] for t in range(chunk)], axis=1)
+        near_row, far_row = row_norms(near), row_norms(far)
+        cross = kernel_block(picked, picked_column, near, near_row)
+        own_near = kernel_block(own, own_column, near, near_row)
+        own_far = kernel_block(own, own_column, far, far_row)
+        beside_near = kernel_block(beside, beside_column, near, near_row)
+        size = own.shape[0]
+        for t in range(chunk):
+            tile_ref[at + t, core] = own_near[:, t * size : (t + 1) * size]
+            tile_ref[at + t, other] = own_far[:, t * size : (t + 1) * size]
+        top = jnp.dot(
+            inverse_ref[:half, :half],
+            cross[:half],
+            precision=highest,
+            preferred_element_type=jnp.float32,
+        )
+        low = jnp.dot(
+            inverse_ref[half:, :], cross, precision=highest, preferred_element_type=jnp.float32
+        )
+        both = jnp.concatenate([top, low], axis=0)
+        gram_part[:half, :] += dot_t(top, both)
+        gram_part[half:, half:] += dot_t(low, low)
+        proj_part[...] += dot_t(near_targets, both)
+        zed_ref[...] += dot_t(own_near, both)
+        zed_part[...] += dot_t(beside_near, both)
+        image_ref[...] += dot_t(near_targets, own_near) + dot_t(far_targets, own_far)
+        squares = near_targets * near_targets + far_targets * far_targets
+        for t in range(chunk):
+            square_ref[...] += squares[:, t * size : (t + 1) * size]
+        return carry
+
+    lax.fori_loop(0, n // 2 // chunk, step, 0)
+    pl.semaphore_wait(barrier, 1)
+    copies = []
+    for k, (src, dst) in enumerate(
+        [
+            (gram_part.at[:half, :], gram_got.at[:half, :]),
+            (gram_part.at[half:, half:], gram_got.at[half:, half:]),
+            (proj_part, proj_got),
+            (zed_part, zed_got),
+        ]
+    ):
+        copy = pltpu.make_async_remote_copy(
+            src_ref=src,
+            dst_ref=dst,
+            send_sem=send_sem.at[k],
+            recv_sem=recv_sem.at[k],
+            device_id=coords(partner, width),
+            device_id_type=MESH,
+        )
+        copy.start()
+        copies.append(copy)
+    square_ref[...] = jnp.broadcast_to(
+        jnp.sum(square_ref[...], axis=1, keepdims=True), square_ref.shape
+    )
+    gram_ref[half:, :half] = jnp.zeros((order - half, half), jnp.float32)
+    copies[0].wait_recv()
+    gram_ref[:half, :] = gram_part[:half, :] + gram_got[:half, :]
+    copies[1].wait_recv()
+    gram_ref[half:, half:] = gram_part[half:, half:] + gram_got[half:, half:]
+    copies[2].wait_recv()
+    proj_ref[...] = proj_part[...] + proj_got[...]
+    copies[3].wait_recv()
+    zed_ref[...] += zed_got[...]
+    for copy in copies:
+        copy.wait_send()
+
+
+def sweep(all_points, all_targets, picked, inverse, n, width):
+    rows, rhs_count, order = all_points.shape[1], all_targets.shape[1], picked.shape[0]
     vmem = pl.BlockSpec(memory_space=pltpu.VMEM)
-    pieces = part.reshape(n, part.shape[0] // n, part.shape[1])
-    summed = pl.pallas_call(
-        functools.partial(reduce_kernel, n, width),
-        out_shape=jax.ShapeDtypeStruct(pieces.shape, pieces.dtype),
-        in_specs=[vmem],
-        out_specs=vmem,
-        scratch_shapes=[pltpu.VMEM((n - 1,) + pieces.shape[1:], pieces.dtype)]
-        + [pltpu.SemaphoreType.DMA] * 4,
-        compiler_params=pltpu.CompilerParams(collective_id=1, has_side_effects=True),
-        name="sum_gram",
-    )(pieces)
-    return summed.reshape(part.shape)
+    f32 = jnp.float32
+    partial = [
+        pltpu.VMEM((order, order), f32),
+        pltpu.VMEM((rhs_count, order), f32),
+        pltpu.VMEM((rows, order), f32),
+    ]
+    factor, wide, tile, *rest = pl.pallas_call(
+        functools.partial(sweep_kernel, n, width),
+        out_shape=[
+            jax.ShapeDtypeStruct(shape, dtype)
+            for shape, dtype in [
+                ((rows, order), jnp.bfloat16),
+                ((rows, order), f32),
+                ((n // 2, 2, rows, rows), f32),
+                ((order, order), f32),
+                ((rhs_count, order), f32),
+                ((rows, order), f32),
+                ((rhs_count, rows), f32),
+                ((rhs_count, rows), f32),
+            ]
+        ],
+        in_specs=[vmem] * 4,
+        out_specs=[vmem] * 8,
+        scratch_shapes=partial * 2 + [pltpu.SemaphoreType.DMA((4,))] * 2,
+        compiler_params=pltpu.CompilerParams(
+            collective_id=1, has_side_effects=True, vmem_limit_bytes=60 * 2**20
+        ),
+        name="sweep_points",
+    )(
+        all_points.reshape((n // 2, 2) + all_points.shape[1:]),
+        all_targets.reshape((n // 2, 2) + all_targets.shape[1:]),
+        picked,
+        inverse,
+    )
+    return [factor, wide, tile.reshape(n, rows, rows)] + rest
 
 
 def cg_kernel(
@@ -288,7 +497,11 @@
     tile_ref,
     rhs_ref,
     wide_ref,
+    zed_ref,
     inverse_ref,
+    proj_ref,
+    image_ref,
+    square_ref,
     sol_ref,
     res_ref,
     dirs,
@@ -298,8 +511,10 @@
     kept_proj,
     kept_squares,
     kept_rz,
+    all_rz,
     dir_send,
     dir_recv,
+    dir_pair,
     put_send,
     put_recv,
     ans_send,
@@ -404,13 +619,7 @@
         only_owners(body)
 
     def solve(proj):
-        half = lax.dot_general(
-            proj,
-            inverse_ref[...],
-            (((1,), (1,)), ((), ())),
-            precision=highest,
-            preferred_element_type=jnp.float32,
-        )
+        half = dot_t(proj, inverse_ref[...])
         coef = jnp.dot(
             half, inverse_ref[...], precision=highest, preferred_element_type=jnp.float32
         )
@@ -425,30 +634,31 @@
     def joined(packed):
         return jnp.concatenate([packed[:, q, :] for q in range(lanes)], axis=1)
 
-    def precondition(residual, k):
-        packed = ans[k]
-        back = lax.dot_general(
-            joined(packed),
-            wide_ref[...],
-            (((1,), (1,)), ((), ())),
-            precision=highest,
-            preferred_element_type=jnp.float32,
-        )
-        return (residual - back) * (1.0 / noise_level)
+    def preconditioned(coef, residual, applied):
+        direction = (residual - dot_t(coef, wide_ref[...])) * (1.0 / noise_level)
+        image = (applied - dot_t(coef, zed_ref[...])) * (1.0 / noise_level)
+        return direction, image
+
+    def multiplied(k, image):
+        def one(j, acc):
+            return acc + dot_t(dirs[k, j], tile_ref[j])
+
+        return lax.fori_loop(0, n, one, noise_level * image, unroll=4)
 
     residual = rhs_ref[...]
+    applied = image_ref[...]
     solution = jnp.zeros_like(residual)
-    to_owners(0, project(residual), [wide_sum(residual * residual)])
-
-    def first_answer():
-        total = collect(0)
-        proj = joined(total)
-        squares = total[:, lanes, :]
-        coef, covered = solve(proj)
-        kept_proj[...] = proj
-        kept_squares[...] = squares
-        kept_rz[...] = (squares - covered) * (1.0 / noise_level)
-        answer(0, split(coef))
+    coef, covered = solve(proj_ref[...])
+    all_rz[...] = (square_ref[...] - covered) * (1.0 / noise_level)
+    direction, image = preconditioned(coef, residual, applied)
+
+    def keep_own():
+        rows = pl.ds(me * per, per)
+        kept_proj[...] = proj_ref[rows, :]
+        kept_squares[...] = square_ref[rows, :]
+        kept_rz[...] = all_rz[rows, :]
+
+    only_owners(keep_own)
 
     def later_answer(k, last):
         total = collect(k)
@@ -468,58 +678,55 @@
         kept_rz[...] = rz
         answer(k, split(coef) + [size, rz / rz_before])
 
-    only_owners(first_answer)
-    await_answer(0)
-    direction = precondition(residual, 0)
-
-    for step_index in range(ITERS):
-        last = step_index + 1 == ITERS
-        dirs[step_index, me] = direction
-        spread(
-            n,
-            width,
-            me,
-            lambda peer, i: dirs.at[step_index, me],
-            lambda peer, i: dirs.at[step_index, me],
-            dir_send.at[step_index],
-            dir_recv.at[step_index],
-        )
-        drain(dirs.at[step_index, pl.ds(0, n - 1)], dir_recv.at[step_index])
-
-        def multiply(j, acc):
-            return acc + jnp.dot(
-                dirs[step_index, j],
-                tile_ref[j],
-                precision=highest,
-                preferred_element_type=jnp.float32,
-            )
-
-        image = lax.fori_loop(0, n, multiply, noise_level * direction, unroll=4)
-        k = step_index + 1
+    relays = []
+    for k in range(ITERS):
+        last = k + 1 == ITERS
         sums = [wide_sum(direction * image)]
         if last:
             to_owners(k, jnp.zeros((rhs_count, order), jnp.float32), sums)
         else:
+            dirs[k, me] = image
+            relay = Relay(
+                n,
+                width,
+                me,
+                dirs.at[k],
+                dirs.at[k, me],
+                dir_send.at[k],
+                dir_recv.at[k],
+                dir_pair.at[k],
+            )
+            relays.append(relay)
+            relay.start()
             to_owners(
                 k, project(image), sums + [wide_sum(residual * image), wide_sum(image * image)]
             )
+            relay.relay_lines()
         only_owners(functools.partial(later_answer, k, last))
+        if not last:
+            relay.relay_plane()
+            relay.finish()
+            twice = multiplied(k, image)
         await_answer(k)
         size = ans[k, :, lanes, :]
         solution = solution + size * direction
         residual = residual - size * image
         if not last:
-            direction = precondition(residual, k) + ans[k, :, lanes + 1, :] * direction
+            ratio = ans[k, :, lanes + 1, :]
+            applied = applied - size * twice
+            fresh, fresh_image = preconditioned(joined(ans[k]), residual, applied)
+            direction = fresh + ratio * direction
+            image = fresh_image + ratio * image
     sol_ref[...] = solution
     res_ref[...] = residual
-    for step_index in range(ITERS):
-        drain(dirs.at[step_index, pl.ds(0, n - 1)], dir_send.at[step_index])
-    for k in range(ITERS + 1):
+    for relay in relays:
+        relay.finish_sends()
+    for k in range(ITERS):
         finish_put(k)
         finish_answer(k)
 
 
-def solve_cg(tile, targets_t, wide_factor, inverse, n, width):
+def solve_cg(tile, targets_t, wide_factor, zed, inverse, proj, image, squares, n, width):
     rhs_count, row_count = targets_t.shape
     owners = min(n, rhs_count)
     per = rhs_count // owners
@@ -530,40 +737,42 @@
     return pl.pallas_call(
         functools.partial(cg_kernel, n, width, owners),
         out_shape=[jax.ShapeDtypeStruct((rhs_count, row_count), f32)] * 2,
-        in_specs=[vmem] * 4,
+        in_specs=[vmem] * 8,
         out_specs=[vmem] * 2,
         scratch_shapes=[
-            pltpu.VMEM((ITERS, n, rhs_count, row_count), f32),
-            pltpu.VMEM((ITERS + 1, rhs_count, rows, LANES), f32),
-            pltpu.VMEM((ITERS + 1, n - 1, per, rows, LANES), f32),
-            pltpu.VMEM((ITERS + 1, rhs_count, rows, LANES), f32),
+            pltpu.VMEM((ITERS - 1, n, rhs_count, row_count), f32),
+            pltpu.VMEM((ITERS, rhs_count, rows, LANES), f32),
+            pltpu.VMEM((ITERS, n - 1, per, rows, LANES), f32),
+            pltpu.VMEM((ITERS, rhs_count, rows, LANES), f32),
             pltpu.VMEM((per, order), f32),
             pltpu.VMEM((per, LANES), f32),
             pltpu.VMEM((per, LANES), f32),
-            pltpu.SemaphoreType.DMA((ITERS,)),
-            pltpu.SemaphoreType.DMA((ITERS,)),
+            pltpu.VMEM((rhs_count, LANES), f32),
+            pltpu.SemaphoreType.DMA((ITERS - 1,)),
+            pltpu.SemaphoreType.DMA((ITERS - 1, n // 2)),
+            pltpu.SemaphoreType.DMA((ITERS - 1,)),
         ]
-        + [pltpu.SemaphoreType.DMA((ITERS + 1,))] * 4,
-        compiler_params=pltpu.CompilerParams(collective_id=2, has_side_effects=True),
+        + [pltpu.SemaphoreType.DMA((ITERS,))] * 4,
+        compiler_params=pltpu.CompilerParams(
+            collective_id=2, has_side_effects=True, vmem_limit_bytes=60 * 2**20
+        ),
         name="conjugate_gradients",
-    )(tile.reshape(n, row_count, row_count), targets_t, wide_factor, inverse)
+    )(tile, targets_t, wide_factor, zed, inverse, proj, image, squares)
 
 
 def per_device(n, width, points, targets, pivots):
-    piv_count = pivots.shape[1]
-    all_points = gather_all(points, n, width)
-    all_points = all_points.reshape(-1, points.shape[1])
-    picked = all_points[pivots.reshape(-1)]
-    wide_factor = build_factor(points, picked)
-    factor = wide_factor.astype(jnp.bfloat16)
-    local_gram = lax.dot_general(
-        wide_factor, wide_factor, (((0,), (0,)), ((), ())), precision=highest
-    )
-    order = 2 * piv_count
-    gram = unpack_upper(reduce_all(pack_upper(local_gram), n, width), order)
-    inverse = chol_inverse(gram + noise_level * jnp.eye(order, dtype=jnp.float32))
-    tile = kernel_block(all_points, squared_norms(all_points), points, squared_norms(points))
-    solution_t, residual_t = solve_cg(tile, targets.T, wide_factor, inverse, n, width)
+    targets_t = targets.T
+    all_points, all_targets = gather_all(points, targets_t, n, width)
+    picked = all_points.reshape(-1, points.shape[1])[pivots.reshape(-1)]
+    order = picked.shape[0]
+    inverse = chol_inverse(pivot_kernel, picked, order, "pivot_inverse")
+    factor, wide, tile, gram, proj, zed, image, squares = sweep(
+        all_points, all_targets, picked, inverse, n, width
+    )
+    gram_inverse = chol_inverse(gram_kernel, gram, order, "gram_inverse")
+    solution_t, residual_t = solve_cg(
+        tile, targets_t, wide, zed, gram_inverse, proj, image, squares, n, width
+    )
     return (factor, solution_t.T, residual_t.T)
 
 

time: 242 us -> 160 us (0.66)
  Pallas kernels: 222 us -> 151 us
  matrix products: 7.56 us -> 0 us
  other arithmetic: 4.87 us -> 0.01 us
    pallas_call x1, Pallas kernels: 115 us -> 49.9 us  [solve_cg(): pl.pallas_call(functools.partial(cg_kernel, n, width, owners), out_shape=...]
    dot_general x5 -> x0, matrix products: 7.56 us -> none  [the longest x3 3.49 us: kernel_block(): lax.dot_general(left_rows, right_rows, (((1,), (1,)), ((), ())), preferre...]
    pallas_call x4, Pallas kernels: 107 us -> 102 us  [the longest x2 45 us: chol_inverse(): pl.pallas_call(kernel, out_shape=jax.ShapeDtypeStruct((order, order), jnp...]
    reduce_sum x3 -> x0, other arithmetic: 2.91 us -> none  [squared_norms(): return jnp.sum(wide_rows * wide_rows, axis=1)]
where the time goes in v1:
time: 160 us; the launch traced here: 159 us
  Pallas kernels  151 us (94%)
  local copies, waits for them, and re-layouts  7.02 us (4%)
    pallas_call x1, Pallas kernels, solve_cg(): pl.pallas_call(functools.partial(cg_kernel, n, width, owners), out_shape=...  49.9 us
    pallas_call x2, Pallas kernels, chol_inverse(): pl.pallas_call(kernel, out_shape=jax.ShapeDtypeStruct((order, order), jnp...  45 us
    pallas_call x1, Pallas kernels, sweep(): pl.pallas_call(functools.partial(sweep_kernel, n, width), out_shape=[jax....  35.3 us
    pallas_call x1, Pallas kernels, gather_all(): pl.pallas_call(functools.partial(gather_kernel, n, width), out_shape=[jax...  21.2 us
    unnamed x6, local copies, waits for them, and re-layouts  3.99 us

profile of v1, /device:TPU:0, one launch (start us, length us, event | category | flops | bytes accessed | tf_op | source)
XLA Modules:
  0.0 159.1 jit_solution(12386821651572673259)
XLA Ops:
  0.6 0.7 copy.6
  1.3 21.2 %gather_points.1 = (bf16[32,128,128]{2,1,0:T(8,128)(2,1)}, f32[32,32,128]{2,1,0:T(8,128)}) custom-call(bf16[128,128]{1,0:T(8,128)(2,1)} %points_ref.1, f32[32,128]{1,0:T(8,128)} %bitcast.16), custom_call_target="tpu_custom_call" | custom-call | tf_op jit(solution)/shard_map/gather_points/pallas_call | solution.py:309
  22.5 3.0 %gather_fusion = bf16[512,128]{1,0:T(8,128)(2,1)} fusion(bf16[4096,128]{1,0:T(8,128)(2,1)} %bitcast.12, s32[1024]{0:T(1024)S(1)} %pad_clamp_fusion), kind=kCustom, calls=%fused_computation | custom fusion | bytes 264192 | tf_op jit(solution)/shard_map/gather | solution.py:766
  25.6 22.5 %pivot_inverse.1.inverse_ref = f32[512,512]{1,0:T(8,128)} custom-call(bf16[512,128]{1,0:T(8,128)(2,1)} %gather_fusion), custom_call_target="tpu_custom_call" | custom-call | tf_op jit(solution)/shard_map/pivot_inverse/pallas_call | solution.py:155
  48.1 35.3 %sweep_points.1 = (bf16[128,512]{1,0:T(8,128)(2,1)}, f32[128,512]{1,0:T(8,128)}, f32[16,2,128,128]{3,2,1,0:T(8,128)}, f32[512,512]{1,0:T(8,128)}, f32[32,512]{1,...) custom-call(bf16[16,2,128,128]{3,2,1,0:T(8,128)(2,1)} %bitcast.13, ...), custom_call_target="tpu_custom_call" | custom-call | tf_op jit(solution)/shard_map/sweep_points/pallas_call | solution.py:462
  83.4 22.5 %gram_inverse.1.inverse_ref = f32[512,512]{1,0:T(8,128)} custom-call(f32[512,512]{1,0:T(8,128)} %get-tuple-element.21.gram_ref), custom_call_target="tpu_custom_call" | custom-call | tf_op jit(solution)/shard_map/gram_inverse/pallas_call | solution.py:155
  105.9 0.0 copy-start
  105.9 49.9 %conjugate_gradients.1 = (f32[32,128]{1,0:T(8,128)}, f32[32,128]{1,0:T(8,128)}) custom-call(f32[32,128,128]{2,1,0:T(8,128)} %bitcast.14, f32[32,128]{1,0:T(8,128)} %bitcast.17, f32[128,512]{1,0:T(8,128)} %get-tuple-element.19.wide_ref, f32[128,512]{1,0:T(8,128)} %get-tuple-element.20.zed_ref, f32[512,512]{1,0:T(8,128)} %gram_inverse.1.inverse_ref, ...), custom_call_target="tpu_custom_call" | custom-call | tf_op jit(solution)/shard_map/conjugate_gradients/pallas_call | solution.py:737
  155.8 0.0 copy-done
  155.8 0.7 copy.10
  156.5 1.3 copy.11
  157.8 1.3 copy.12
  (2 shorter events, 0.0 us)
Async XLA Ops:
  105.9 49.9 %copy-start = (bf16[128,512]{1,0:T(8,128)(2,1)S(1)}, bf16[128,512]{1,0:T(8,128)(2,1)}, u32[]{:S(2)}) copy-start(bf16[128,512]{1,0:T(8,128)(2,1)} %get-tuple-element.30) | copy-start | bytes 393220

commit v2 on v1

--- a/solution.py
+++ b/solution.py
@@ -48,44 +48,81 @@
 
 def lower_inverse_rows(rows):
     count = len(rows)
+    group = max(count // 2, 1)
     lane = lax.broadcasted_iota(jnp.int32, (8, LANES), 1)
     sub = lax.broadcasted_iota(jnp.int32, (8, LANES), 0)
 
     def full_of(values):
         return jnp.broadcast_to(values, (8, LANES))
 
+    def columns(row, base):
+        return [full_of(row[:, base + c : base + c + 1]) for c in range(8)]
+
     rows = list(rows)
     done = []
-    for p in range(count):
-        base = 8 * p
-        inside = (lane >= base) & (lane < base + 8)
-        cols = [full_of(rows[p][:, base + c : base + c + 1]) for c in range(8)]
-        forward = jnp.where(inside, jnp.where(lane == sub + base, 1.0, 0.0), rows[p])
-        pivots = jnp.ones((8, LANES), jnp.float32)
-        recips, spread_rows, coefs = [], [], []
-        for j in range(8):
-            pivot = full_of(cols[j][j : j + 1])
-            recip = 1.0 / pivot
-            pivots = jnp.where(sub == j, pivot, pivots)
-            below = jnp.where(sub > j, cols[j] * recip, 0.0)
-            spread_row = full_of(forward[j : j + 1])
-            forward = forward - below * spread_row
-            coef = {c: full_of(cols[c][j : j + 1]) for c in range(j + 1, 8)}
-            for c in range(j + 1, 8):
-                cols[c] = cols[c] - below * coef[c]
-            recips.append(recip)
-            spread_rows.append(spread_row)
-            coefs.append(coef)
-        done.append(jnp.where(lane <= sub + base, forward, 0.0) * lax.rsqrt(pivots))
-        for v in range(p + 1, count):
-            own = [full_of(rows[v][:, base + c : base + c + 1]) for c in range(8)]
-            new = jnp.where(inside, 0.0, rows[v])
+    for start in range(0, count, group):
+        end = start + group
+        whole = []
+        ahead = columns(rows[start], 8 * start)
+        for p in range(start, end):
+            base = 8 * p
+            inside = (lane >= base) & (lane < base + 8)
+            cols = ahead
+            forward = jnp.where(inside, jnp.where(lane == sub + base, 1.0, 0.0), rows[p])
+            pivots = jnp.ones((8, LANES), jnp.float32)
+            recips, spread_rows, coefs = [], [], []
+            more = p + 1 < end
+            if more:
+                own = columns(rows[p + 1], base)
+                ahead = columns(rows[p + 1], base + 8)
+                following = jnp.where(inside, 0.0, rows[p + 1])
             for j in range(8):
-                multiplier = own[j] * recips[j]
-                new = new - multiplier * spread_rows[j]
+                pivot = full_of(cols[j][j : j + 1])
+                recip = 1.0 / pivot
+                pivots = jnp.where(sub == j, pivot, pivots)
+                below = jnp.where(sub > j, cols[j] * recip, 0.0)
+                spread_row = full_of(forward[j : j + 1])
+                forward = forward - below * spread_row
+                coef = {c: full_of(cols[c][j : j + 1]) for c in range(j + 1, 8)}
                 for c in range(j + 1, 8):
-                    own[c] = own[c] - multiplier * coefs[j][c]
-            rows[v] = new
+                    cols[c] = cols[c] - below * coef[c]
+                if more:
+                    multiplier = own[j] * recip
+                    for c in range(j + 1, 8):
+                        own[c] = own[c] - multiplier * coef[c]
+                    for c in range(8):
+                        ahead[c] = ahead[c] - multiplier * full_of(own[j][c : c + 1])
+                    following = following - multiplier * spread_row
+                recips.append(recip)
+                spread_rows.append(spread_row)
+                coefs.append(coef)
+            scaled = forward * lax.rsqrt(pivots)
+            lower = lane <= sub + base
+            done.append(jnp.where(lower, scaled, 0.0))
+            whole.append(jnp.where(lower | (lane >= 8 * end), scaled, 0.0))
+            if more:
+                rows[p + 1] = following
+            for v in range(p + 2, end):
+                own_v = columns(rows[v], base)
+                new = jnp.where(inside, 0.0, rows[v])
+                for j in range(8):
+                    multiplier = own_v[j] * recips[j]
+                    new = new - multiplier * spread_rows[j]
+                    for c in range(j + 1, 8):
+                        own_v[c] = own_v[c] - multiplier * coefs[j][c]
+                rows[v] = new
+        if end < count:
+            side = jnp.concatenate(whole, axis=0)
+            both = lax.dot_general(
+                side,
+                side,
+                (((0,), (0,)), ((), ())),
+                precision=highest,
+                preferred_element_type=jnp.float32,
+            )
+            inside = (lane >= 8 * start) & (lane < 8 * end)
+            for v in range(end, count):
+                rows[v] = jnp.where(inside, 0.0, rows[v]) - both[8 * v : 8 * v + 8]
     return done
 
 
@@ -337,12 +374,10 @@
     zed_ref,
     image_ref,
     square_ref,
-    gram_part,
-    proj_part,
-    zed_part,
-    gram_got,
-    proj_got,
-    zed_got,
+    left_part,
+    right_part,
+    left_got,
+    right_got,
     send_sem,
     recv_sem,
 ):
@@ -373,8 +408,7 @@
     own_targets = targets_ref[pair, core]
     image_ref[...] = noise_level * own_targets
     square_ref[...] = jnp.zeros_like(square_ref)
-    zed_ref[...] = noise_level * wide
-    for ref in (gram_part, proj_part, zed_part):
+    for ref in (left_part, right_part):
         ref[...] = jnp.zeros_like(ref)
 
     def step(i, carry):
@@ -392,21 +426,22 @@
         for t in range(chunk):
             tile_ref[at + t, core] = own_near[:, t * size : (t + 1) * size]
             tile_ref[at + t, other] = own_far[:, t * size : (t + 1) * size]
-        top = jnp.dot(
-            inverse_ref[:half, :half],
+        first = jnp.dot(
+            inverse_ref[:, :half],
             cross[:half],
             precision=highest,
             preferred_element_type=jnp.float32,
         )
-        low = jnp.dot(
-            inverse_ref[half:, :], cross, precision=highest, preferred_element_type=jnp.float32
+        top = first[:half]
+        low = first[half:] + jnp.dot(
+            inverse_ref[half:, half:],
+            cross[half:],
+            precision=highest,
+            preferred_element_type=jnp.float32,
         )
-        both = jnp.concatenate([top, low], axis=0)
-        gram_part[:half, :] += dot_t(top, both)
-        gram_part[half:, half:] += dot_t(low, low)
-        proj_part[...] += dot_t(near_targets, both)
-        zed_ref[...] += dot_t(own_near, both)
-        zed_part[...] += dot_t(beside_near, both)
+        extra = [own_near, beside_near, near_targets]
+        left_part[...] += dot_t(jnp.concatenate([top] + extra, axis=0), top)
+        right_part[...] += dot_t(jnp.concatenate([top, low] + extra, axis=0), low)
         image_ref[...] += dot_t(near_targets, own_near) + dot_t(far_targets, own_far)
         squares = near_targets * near_targets + far_targets * far_targets
         for t in range(chunk):
@@ -415,37 +450,36 @@
 
     lax.fori_loop(0, n // 2 // chunk, step, 0)
     pl.semaphore_wait(barrier, 1)
+    size = own.shape[0]
+    sides = [(left_part, left_got, half, 0), (right_part, right_got, order, half)]
     copies = []
-    for k, (src, dst) in enumerate(
-        [
-            (gram_part.at[:half, :], gram_got.at[:half, :]),
-            (gram_part.at[half:, half:], gram_got.at[half:, half:]),
-            (proj_part, proj_got),
-            (zed_part, zed_got),
-        ]
-    ):
-        copy = pltpu.make_async_remote_copy(
-            src_ref=src,
-            dst_ref=dst,
-            send_sem=send_sem.at[k],
-            recv_sem=recv_sem.at[k],
-            device_id=coords(partner, width),
-            device_id_type=MESH,
-        )
-        copy.start()
-        copies.append(copy)
+    for part, got, tall, _ in sides:
+        for rows in (pl.ds(0, tall), pl.ds(tall + size, part.shape[0] - tall - size)):
+            copy = pltpu.make_async_remote_copy(
+                src_ref=part.at[rows],
+                dst_ref=got.at[rows],
+                send_sem=send_sem.at[len(copies)],
+                recv_sem=recv_sem.at[len(copies)],
+                device_id=coords(partner, width),
+                device_id_type=MESH,
+            )
+            copy.start()
+            copies.append(copy)
     square_ref[...] = jnp.broadcast_to(
         jnp.sum(square_ref[...], axis=1, keepdims=True), square_ref.shape
     )
     gram_ref[half:, :half] = jnp.zeros((order - half, half), jnp.float32)
-    copies[0].wait_recv()
-    gram_ref[:half, :] = gram_part[:half, :] + gram_got[:half, :]
-    copies[1].wait_recv()
-    gram_ref[half:, half:] = gram_part[half:, half:] + gram_got[half:, half:]
-    copies[2].wait_recv()
-    proj_ref[...] = proj_part[...] + proj_got[...]
-    copies[3].wait_recv()
-    zed_ref[...] += zed_got[...]
+    for copy in copies:
+        copy.wait_recv()
+    for part, got, tall, at in sides:
+        lanes = slice(at, at + part.shape[1])
+        gram_ref[:tall, lanes] = part[:tall] + got[:tall]
+        zed_ref[:, lanes] = (
+            noise_level * wide_ref[:, lanes]
+            + part[tall : tall + size]
+            + got[tall + size : tall + 2 * size]
+        )
+        proj_ref[:, lanes] = part[tall + 2 * size :] + got[tall + 2 * size :]
     for copy in copies:
         copy.wait_send()
 
@@ -454,10 +488,11 @@
     rows, rhs_count, order = all_points.shape[1], all_targets.shape[1], picked.shape[0]
     vmem = pl.BlockSpec(memory_space=pltpu.VMEM)
     f32 = jnp.float32
+    half = order // 2
+    extra = 2 * rows + rhs_count
     partial = [
-        pltpu.VMEM((order, order), f32),
-        pltpu.VMEM((rhs_count, order), f32),
-        pltpu.VMEM((rows, order), f32),
+        pltpu.VMEM((half + extra, half), f32),
+        pltpu.VMEM((order + extra, order - half), f32),
     ]
     factor, wide, tile, *rest = pl.pallas_call(
         functools.partial(sweep_kernel, n, width),

time: 160 us -> 141 us (0.88)
  Pallas kernels: 151 us -> 133 us
    pallas_call x2, Pallas kernels: 45 us -> 34.5 us  [chol_inverse(): pl.pallas_call(kernel, out_shape=jax.ShapeDtypeStruct((order, order), jnp...]
    pallas_call x1, Pallas kernels: 35.3 us -> 27.8 us  [sweep(): pl.pallas_call(functools.partial(sweep_kernel, n, width), out_shape=[jax....]
where the time goes in v2:
time: 141 us
  Pallas kernels  133 us (94%)
  local copies, waits for them, and re-layouts  7.02 us (5%)
    pallas_call x1, Pallas kernels, solve_cg(): pl.pallas_call(functools.partial(cg_kernel, n, width, owners), out_shape=...  49.9 us
    pallas_call x2, Pallas kernels, chol_inverse(): pl.pallas_call(kernel, out_shape=jax.ShapeDtypeStruct((order, order), jnp...  34.5 us
    pallas_call x1, Pallas kernels, sweep(): pl.pallas_call(functools.partial(sweep_kernel, n, width), out_shape=[jax....  27.8 us
    pallas_call x1, Pallas kernels, gather_all(): pl.pallas_call(functools.partial(gather_kernel, n, width), out_shape=[jax...  21.2 us
    unnamed x6, local copies, waits for them, and re-layouts  3.99 us
    gather x1, local copies, waits for them, and re-layouts, per_device(): picked = all_points.reshape(-1, points.shape[1])[pivots.reshape(-1)]  3.03 us

profile of v2, /device:TPU:0, one launch (start us, length us, event | category | flops | bytes accessed | tf_op | source)
XLA Modules:
  0.0 141.0 jit_solution(13992334379787985699)
XLA Ops:
  0.6 0.7 copy.6
  1.3 21.2 %gather_points.1 = (bf16[32,128,128]{2,1,0:T(8,128)(2,1)}, f32[32,32,128]{2,1,0:T(8,128)}) custom-call(bf16[128,128]{1,0:T(8,128)(2,1)} %points_ref.1, f32[32,128]{1,0:T(8,128)} %bitcast.16), custom_call_target="tpu_custom_call" | custom-call | tf_op jit(solution)/shard_map/gather_points/pallas_call | solution.py:346
  22.5 3.0 %gather_fusion = bf16[512,128]{1,0:T(8,128)(2,1)} fusion(bf16[4096,128]{1,0:T(8,128)(2,1)} %bitcast.12, s32[1024]{0:T(1024)S(1)} %pad_clamp_fusion), kind=kCustom, calls=%fused_computation | custom fusion | bytes 264192 | tf_op jit(solution)/shard_map/gather | solution.py:801
  25.6 17.2 %pivot_inverse.1.inverse_ref = f32[512,512]{1,0:T(8,128)} custom-call(bf16[512,128]{1,0:T(8,128)(2,1)} %gather_fusion), custom_call_target="tpu_custom_call" | custom-call | tf_op jit(solution)/shard_map/pivot_inverse/pallas_call | solution.py:192
  42.8 27.8 %sweep_points.1 = (bf16[128,512]{1,0:T(8,128)(2,1)}, f32[128,512]{1,0:T(8,128)}, f32[16,2,128,128]{3,2,1,0:T(8,128)}, f32[512,512]{1,0:T(8,128)}, f32[32,512]{1,...) custom-call(bf16[16,2,128,128]{3,2,1,0:T(8,128)(2,1)} %bitcast.13, ...), custom_call_target="tpu_custom_call" | custom-call | tf_op jit(solution)/shard_map/sweep_points/pallas_call | solution.py:497
  70.6 17.2 %gram_inverse.1.inverse_ref = f32[512,512]{1,0:T(8,128)} custom-call(f32[512,512]{1,0:T(8,128)} %get-tuple-element.21.gram_ref), custom_call_target="tpu_custom_call" | custom-call | tf_op jit(solution)/shard_map/gram_inverse/pallas_call | solution.py:192
  87.8 0.0 copy-start
  87.8 49.9 %conjugate_gradients.1 = (f32[32,128]{1,0:T(8,128)}, f32[32,128]{1,0:T(8,128)}) custom-call(f32[32,128,128]{2,1,0:T(8,128)} %bitcast.14, f32[32,128]{1,0:T(8,128)} %bitcast.17, f32[128,512]{1,0:T(8,128)} %get-tuple-element.19.wide_ref, f32[128,512]{1,0:T(8,128)} %get-tuple-element.20.zed_ref, f32[512,512]{1,0:T(8,128)} %gram_inverse.1.inverse_ref, ...), custom_call_target="tpu_custom_call" | custom-call | tf_op jit(solution)/shard_map/conjugate_gradients/pallas_call | solution.py:772
  137.7 0.0 copy-done
  137.7 0.7 copy.10
  138.4 1.3 copy.11
  139.7 1.3 copy.12
  (2 shorter events, 0.0 us)
Async XLA Ops:
  87.8 49.9 %copy-start = (bf16[128,512]{1,0:T(8,128)(2,1)S(1)}, bf16[128,512]{1,0:T(8,128)(2,1)}, u32[]{:S(2)}) copy-start(bf16[128,512]{1,0:T(8,128)(2,1)} %get-tuple-element.30) | copy-start | bytes 393220

commit v3 on v2

--- a/solution.py
+++ b/solution.py
@@ -126,7 +126,7 @@
     return done
 
 
-def invert_lower(work, out_ref):
+def invert_lower(work, out_ref, beside=None):
     order = work.shape[0]
     blocks = order // LANES
     row_at = lax.broadcasted_iota(jnp.int32, (LANES, LANES), 0)
@@ -163,6 +163,8 @@
             return inner
 
         lax.fori_loop(j + 1, blocks, below, 0)
+        if beside is not None:
+            beside(j)
         return carry
 
     lax.fori_loop(0, blocks, one_block, 0)
@@ -174,12 +176,55 @@
     return matrix + jnp.where(row_at == col_at, level, 0.0)
 
 
-def pivot_kernel(picked_ref, out_ref, work):
-    picked = picked_ref[...]
+def pivot_kernel(
+    n, width, picked_ref, targets_ref, out_ref, all_targets, work, send_sem, recv_sems, pair_sem
+):
+    me = here(width)
+    hello(n, width, me)
+    all_targets[me] = targets_ref[...]
+    relay = Relay(
+        n, width, me, all_targets, all_targets.at[me], send_sem, recv_sems, pair_sem
+    )
+    picked = picked_ref[...].astype(jnp.bfloat16)
     work[...] = shifted(
         kernel_block(picked, column_norms(picked), picked, row_norms(picked)), jitter_level
     )
-    invert_lower(work, out_ref)
+
+    def begin():
+        all_here(n)
+        relay.start()
+
+    def beside(j):
+        pl.when(j == 0)(begin)
+        pl.when(j == 1)(relay.relay_lines)
+        pl.when(j == 2)(relay.relay_plane)
+
+    invert_lower(work, out_ref, beside)
+    relay.finish()
+    relay.finish_sends()
+
+
+def pivot_inverse(picked, targets_t, n, width):
+    order = picked.shape[0]
+    vmem = pl.BlockSpec(memory_space=pltpu.VMEM)
+    f32 = jnp.float32
+    return pl.pallas_call(
+        functools.partial(pivot_kernel, n, width),
+        out_shape=[
+            jax.ShapeDtypeStruct((order, order), f32),
+            jax.ShapeDtypeStruct((n,) + targets_t.shape, f32),
+        ],
+        in_specs=[vmem] * 2,
+        out_specs=[vmem] * 2,
+        scratch_shapes=[
+            pltpu.VMEM((order, order), f32),
+            pltpu.SemaphoreType.DMA,
+            pltpu.SemaphoreType.DMA((n // 2,)),
+            pltpu.SemaphoreType.DMA,
+        ],
+        compiler_params=pltpu.CompilerParams(collective_id=3, has_side_effects=True),
+        name="pivot_inverse",
+    )(picked, targets_t)
 
 
 def gram_kernel(gram_ref, out_ref, work):
@@ -187,16 +232,16 @@
     invert_lower(work, out_ref)
 
 
-def chol_inverse(kernel, operand, order, name):
+def gram_inverse(gram):
     vmem = pl.BlockSpec(memory_space=pltpu.VMEM)
     return pl.pallas_call(
-        kernel,
-        out_shape=jax.ShapeDtypeStruct((order, order), jnp.float32),
+        gram_kernel,
+        out_shape=jax.ShapeDtypeStruct(gram.shape, jnp.float32),
         in_specs=[vmem],
         out_specs=vmem,
-        scratch_shapes=[pltpu.VMEM((order, order), jnp.float32)],
-        name=name,
-    )(operand)
+        scratch_shapes=[pltpu.VMEM(gram.shape, jnp.float32)],
+        name="gram_inverse",
+    )(gram)
 
 
 def here(width):
@@ -207,18 +252,21 @@
     return (lax.div(index, width), lax.rem(index, width))
 
 
-def greet(n, width, me):
+def hello(n, width, me):
     barrier = pltpu.get_barrier_semaphore()
 
-    def hello(i, carry):
+    def one(i, carry):
         peer = lax.rem(me + i, n)
         pl.semaphore_signal(
             barrier, inc=1, device_id=coords(peer, width), device_id_type=MESH
         )
         return carry
 
-    lax.fori_loop(1, n, hello, 0)
-    pl.semaphore_wait(barrier, n - 1)
+    lax.fori_loop(1, n, one, 0)
+
+
+def all_here(n):
+    pl.semaphore_wait(pltpu.get_barrier_semaphore(), n - 1)
 
 
 def spread(n, width, me, src, dst, send_sem, recv_sem):
@@ -293,8 +341,8 @@
 
         lax.fori_loop(1, self.lines, one, 0)
 
-    def relay_plane(self):
-        for q in range(2, self.plane, 2):
+    def relay_plane(self, *offsets):
+        for q in offsets or range(2, self.plane, 2):
 
             def one(i, carry, q=q):
                 source = lax.rem(flip(self.me, q) - self.plane * i + self.n, self.n)
@@ -313,50 +361,84 @@
 
 
 def gather_kernel(
-    n, width, points_ref, targets_ref, all_points, all_targets, send_sem, recv_sems, pair_sem, own_sem
+    n,
+    width,
+    points_ref,
+    pivots_ref,
+    all_points,
+    picked_ref,
+    send_sem,
+    recv_sems,
+    pair_sem,
+    own_sem,
 ):
     me = here(width)
-    keeps = [
-        pltpu.make_async_copy(points_ref, all_points.at[me], own_sem.at[0]),
-        pltpu.make_async_copy(targets_ref, all_targets.at[me], own_sem.at[1]),
-    ]
-    for keep in keeps:
-        keep.start()
-    greet(n, width, me)
-    relays = [
-        Relay(n, width, me, blocks, own, send_sem.at[k], recv_sems.at[k], pair_sem.at[k])
-        for k, (blocks, own) in enumerate([(all_points, points_ref), (all_targets, targets_ref)])
-    ]
-    for relay in relays:
-        relay.start()
-    for relay in relays:
-        relay.relay_lines()
-    for relay in relays:
-        relay.relay_plane()
-    for relay in relays:
-        relay.finish()
-    for relay in relays:
-        relay.finish_sends()
-    for keep in keeps:
-        keep.wait()
-
-
-def gather_all(points, targets_t, n, width):
+    hello(n, width, me)
+    keep = pltpu.make_async_copy(points_ref, all_points.at[me], own_sem)
+    keep.start()
+    relay = Relay(n, width, me, all_points, points_ref, send_sem, recv_sems, pair_sem)
+    rows = points_ref.shape[0]
+    order = picked_ref.shape[0]
+    pivots = pivots_ref[...].astype(jnp.float32)
+    in_row = jnp.concatenate([pivots[k : k + 1] for k in range(pivots.shape[0])], axis=1)
+    in_column = jnp.broadcast_to(in_row, (8, order)).T
+    chosen = jnp.broadcast_to(in_column[:, 0:1], (order, rows))
+    row_at = lax.broadcasted_iota(jnp.int32, (order, rows), 1).astype(jnp.float32)
+    together = min(4, relay.lines)
+    picked_ref[...] = jnp.zeros_like(picked_ref)
+    all_here(n)
+    relay.start()
+
+    def pick(group):
+        def one(i, carry):
+            sources = [group + relay.plane * (together * i + t) for t in range(together)]
+            hits = [
+                jnp.where(chosen - (rows * source).astype(jnp.float32) == row_at, 1.0, 0.0).astype(jnp.bfloat16)
+                for source in sources
+            ]
+            found = jnp.concatenate([all_points[source] for source in sources], axis=0)
+            picked_ref[...] += jnp.dot(
+                jnp.concatenate(hits, axis=1), found, preferred_element_type=jnp.float32
+            )
+            return carry
+
+        lax.fori_loop(0, relay.lines // together, one, 0)
+
+    def low(bits):
+        return lax.rem(flip(me, bits), relay.plane)
+
+    relay.relay_lines()
+    keep.wait()
+    pick(low(0))
+    for q in range(2, relay.plane, 2):
+        relay.relay_plane(q)
+        pick(low(q))
+    relay.finish()
+    for q in range(0, relay.plane, 2):
+        pick(low(q + 1))
+    relay.finish_sends()
+
+
+def gather_all(points, pivots, n, width):
     vmem = pl.BlockSpec(memory_space=pltpu.VMEM)
+    order = pivots.shape[0] * pivots.shape[1]
     return pl.pallas_call(
         functools.partial(gather_kernel, n, width),
-        out_shape=[jax.ShapeDtypeStruct((n,) + v.shape, v.dtype) for v in (points, targets_t)],
+        out_shape=[
+            jax.ShapeDtypeStruct((n,) + points.shape, points.dtype),
+            jax.ShapeDtypeStruct((order, points.shape[1]), jnp.float32),
+        ],
         in_specs=[vmem] * 2,
         out_specs=[vmem] * 2,
         scratch_shapes=[
-            pltpu.SemaphoreType.DMA((2,)),
-            pltpu.SemaphoreType.DMA((2, n // 2)),
-            pltpu.SemaphoreType.DMA((2,)),
-            pltpu.SemaphoreType.DMA((2,)),
+            pltpu.SemaphoreType.DMA,
+            pltpu.SemaphoreType.DMA((n // 2,)),
+            pltpu.SemaphoreType.DMA,
+            pltpu.SemaphoreType.DMA,
         ],
         compiler_params=pltpu.CompilerParams(collective_id=0, has_side_effects=True),
         name="gather_points",
-    )(points, targets_t)
+    )(points, pivots)
 
 
 def sweep_kernel(
@@ -366,7 +448,6 @@
     targets_ref,
     picked_ref,
     inverse_ref,
-    factor_ref,
     wide_ref,
     tile_ref,
     gram_ref,
@@ -390,7 +471,7 @@
     order = inverse_ref.shape[0]
     half = order // 2
     chunk = min(4, n // 2)
-    picked = picked_ref[...]
+    picked = picked_ref[...].astype(jnp.bfloat16)
     picked_column = column_norms(picked)
     own = points_ref[pair, core]
     beside = points_ref[pair, other]
@@ -404,7 +485,6 @@
         axis=1,
     )
     wide_ref[...] = wide
-    factor_ref[...] = wide.astype(jnp.bfloat16)
     own_targets = targets_ref[pair, core]
     image_ref[...] = noise_level * own_targets
     square_ref[...] = jnp.zeros_like(square_ref)
@@ -494,12 +574,11 @@
         pltpu.VMEM((half + extra, half), f32),
         pltpu.VMEM((order + extra, order - half), f32),
     ]
-    factor, wide, tile, *rest = pl.pallas_call(
+    wide, tile, *rest = pl.pallas_call(
         functools.partial(sweep_kernel, n, width),
         out_shape=[
             jax.ShapeDtypeStruct(shape, dtype)
             for shape, dtype in [
-                ((rows, order), jnp.bfloat16),
                 ((rows, order), f32),
                 ((n // 2, 2, rows, rows), f32),
                 ((order, order), f32),
@@ -510,7 +589,7 @@
             ]
         ],
         in_specs=[vmem] * 4,
-        out_specs=[vmem] * 8,
+        out_specs=[vmem] * 7,
         scratch_shapes=partial * 2 + [pltpu.SemaphoreType.DMA((4,))] * 2,
         compiler_params=pltpu.CompilerParams(
             collective_id=1, has_side_effects=True, vmem_limit_bytes=60 * 2**20
@@ -522,7 +601,7 @@
         picked,
         inverse,
     )
-    return [factor, wide, tile.reshape(n, rows, rows)] + rest
+    return [wide, tile.reshape(n, rows, rows)] + rest
 
 
 def cg_kernel(
@@ -547,6 +626,7 @@
     kept_squares,
     kept_rz,
     all_rz,
+    ends,
     dir_send,
     dir_recv,
     dir_pair,
@@ -554,20 +634,22 @@
     put_recv,
     ans_send,
     ans_recv,
+    end_send,
+    end_recv,
 ):
     me = here(width)
     rhs_count, row_count = rhs_ref.shape
     per = rhs_count // owners
     order = wide_ref.shape[1]
     lanes = order // LANES
-    all_own = owners == n
-    greet(n, width, me)
+    first_owner = (n - owners) // 2
+    rank = me - first_owner
+    owning = (rank >= 0) & (rank < owners)
+    own_rows = pl.ds(rank * per, per)
+    hello(n, width, me)
 
     def only_owners(body):
-        if all_own:
-            body()
-        else:
-            pl.when(me < owners)(body)
+        pl.when(owning)(body)
 
     def wide_sum(values):
         return jnp.broadcast_to(jnp.sum(values, axis=1, keepdims=True), (values.shape[0], LANES))
@@ -579,11 +661,13 @@
             put[k, :, lanes + s, :] = value
 
         def push(i, carry):
-            peer = lax.rem(me + i, owners)
-
-            def go():
+            turn = lax.rem(me + i, owners)
+            peer = first_owner + turn
+
+            @pl.when(peer != me)
+            def _():
                 pltpu.make_async_remote_copy(
-                    src_ref=put.at[k, pl.ds(peer * per, per)],
+                    src_ref=put.at[k, pl.ds(turn * per, per)],
                     dst_ref=got.at[k, lax.rem(me - peer + n, n) - 1],
                     send_sem=put_send.at[k],
                     recv_sem=put_recv.at[k],
@@ -591,57 +675,42 @@
                     device_id_type=MESH,
                 ).start()
 
-            if all_own:
-                go()
-            else:
-                pl.when(peer != me)(go)
             return carry
 
-        lax.fori_loop(1 if all_own else 0, owners, push, 0)
+        lax.fori_loop(0, owners, push, 0)
+
+    def drain_others(ref, sem):
+        @pl.when(owning)
+        def _():
+            drain(ref.at[pl.ds(0, (owners - 1) * per)], sem)
+
+        @pl.when(jnp.logical_not(owning))
+        def _():
+            drain(ref, sem)
 
     def finish_put(k):
-        if all_own:
-            drain(put.at[k, pl.ds(0, (owners - 1) * per)], put_send.at[k])
-        else:
-
-            @pl.when(me < owners)
-            def _():
-                drain(put.at[k, pl.ds(0, (owners - 1) * per)], put_send.at[k])
-
-            @pl.when(me >= owners)
-            def _():
-                drain(put.at[k], put_send.at[k])
+        drain_others(put.at[k], put_send.at[k])
 
     def collect(k):
         drain(got.at[k], put_recv.at[k])
-        start = put[k, pl.ds(me * per, per)]
+        start = put[k, own_rows]
         return lax.fori_loop(0, n - 1, lambda i, acc: acc + got[k, i], start)
 
     def answer(k, rows):
         for s, value in enumerate(rows):
-            ans[k, pl.ds(me * per, per), s, :] = value
+            ans[k, own_rows, s, :] = value
         spread(
             n,
             width,
             me,
-            lambda peer, i: ans.at[k, pl.ds(me * per, per)],
-            lambda peer, i: ans.at[k, pl.ds(me * per, per)],
+            lambda peer, i: ans.at[k, own_rows],
+            lambda peer, i: ans.at[k, own_rows],
             ans_send.at[k],
             ans_recv.at[k],
         )
 
     def await_answer(k):
-        if all_own:
-            drain(ans.at[k, pl.ds(0, (owners - 1) * per)], ans_recv.at[k])
-        else:
-
-            @pl.when(me < owners)
-            def _():
-                drain(ans.at[k, pl.ds(0, (owners - 1) * per)], ans_recv.at[k])
-
-            @pl.when(me >= owners)
-            def _():
-                drain(ans.at[k], ans_recv.at[k])
+        drain_others(ans.at[k], ans_recv.at[k])
 
     def finish_answer(k):
         def body():
@@ -688,20 +757,18 @@
     direction, image = preconditioned(coef, residual, applied)
 
     def keep_own():
-        rows = pl.ds(me * per, per)
-        kept_proj[...] = proj_ref[rows, :]
-        kept_squares[...] = square_ref[rows, :]
-        kept_rz[...] = all_rz[rows, :]
+        for t in range(per):
+            row = pl.ds(rank * per + t, 1)
+            kept_proj[t : t + 1, :] = proj_ref[row, :]
+            kept_squares[t : t + 1, :] = square_ref[row, :]
+            kept_rz[t : t + 1, :] = all_rz[row, :]
 
     only_owners(keep_own)
-
-    def later_answer(k, last):
+    all_here(n)
+
+    def later_answer(k):
         total = collect(k)
-        rz_before = kept_rz[...]
-        size = rz_before / total[:, lanes, :]
-        if last:
-            answer(k, [size] * (lanes + 2))
-            return
+        size = kept_rz[...] / total[:, lanes, :]
         along, image_squares = total[:, lanes + 1, :], total[:, lanes + 2, :]
         size_row = jnp.concatenate([size] * lanes, axis=1)
         proj = kept_proj[...] - size_row * joined(total)
@@ -711,59 +778,79 @@
         kept_proj[...] = proj
         kept_squares[...] = squares
         kept_rz[...] = rz
-        answer(k, split(coef) + [size, rz / rz_before])
+        answer(k, split(coef) + [size, rz])
+
+    def last_sums(values):
+        ends[me, 0:1, 0:rhs_count] = dot_t(jnp.ones((8, row_count), jnp.float32), values)[0:1]
+        spread(
+            n,
+            width,
+            me,
+            lambda peer, i: ends.at[me, pl.ds(0, 1)],
+            lambda peer, i: ends.at[me, pl.ds(0, 1)],
+            end_send,
+            end_recv,
+        )
+        others = ends.at[pl.ds(0, n - 1), pl.ds(0, 1)]
+        drain(others, end_recv)
+        total = lax.fori_loop(1, n, lambda i, acc: acc + ends[i, 0:1, :], ends[0, 0:1, :])
+        lane_at = lax.broadcasted_iota(jnp.int32, (rhs_count, LANES), 1)
+        row_at = lax.broadcasted_iota(jnp.int32, (rhs_count, LANES), 0)
+        spread_out = jnp.broadcast_to(total, (rhs_count, LANES))
+        drain(others, end_send)
+        return wide_sum(jnp.where(lane_at == row_at, spread_out, 0.0))
 
     relays = []
-    for k in range(ITERS):
-        last = k + 1 == ITERS
-        sums = [wide_sum(direction * image)]
-        if last:
-            to_owners(k, jnp.zeros((rhs_count, order), jnp.float32), sums)
-        else:
-            dirs[k, me] = image
-            relay = Relay(
-                n,
-                width,
-                me,
-                dirs.at[k],
-                dirs.at[k, me],
-                dir_send.at[k],
-                dir_recv.at[k],
-                dir_pair.at[k],
-            )
-            relays.append(relay)
-            relay.start()
-            to_owners(
-                k, project(image), sums + [wide_sum(residual * image), wide_sum(image * image)]
-            )
-            relay.relay_lines()
-        only_owners(functools.partial(later_answer, k, last))
-        if not last:
-            relay.relay_plane()
-            relay.finish()
-            twice = multiplied(k, image)
+    for k in range(ITERS - 1):
+        dirs[k, me] = image
+        relay = Relay(
+            n,
+            width,
+            me,
+            dirs.at[k],
+            dirs.at[k, me],
+            dir_send.at[k],
+            dir_recv.at[k],
+            dir_pair.at[k],
+        )
+        relays.append(relay)
+        relay.start()
+        to_owners(
+            k,
+            project(image),
+            [wide_sum(direction * image), wide_sum(residual * image), wide_sum(image * image)],
+        )
+        relay.relay_lines()
+        only_owners(functools.partial(later_answer, k))
+        relay.relay_plane()
+        relay.finish()
+        twice = multiplied(k, image)
         await_answer(k)
         size = ans[k, :, lanes, :]
+        rz = ans[k, :, lanes + 1, :]
+        ratio = rz / all_rz[...]
+        all_rz[...] = rz
         solution = solution + size * direction
         residual = residual - size * image
-        if not last:
-            ratio = ans[k, :, lanes + 1, :]
-            applied = applied - size * twice
-            fresh, fresh_image = preconditioned(joined(ans[k]), residual, applied)
-            direction = fresh + ratio * direction
-            image = fresh_image + ratio * image
+        applied = applied - size * twice
+        fresh, fresh_image = preconditioned(joined(ans[k]), residual, applied)
+        direction = fresh + ratio * direction
+        image = fresh_image + ratio * image
+    size = all_rz[...] / last_sums(direction * image)
+    solution = solution + size * direction
+    residual = residual - size * image
     sol_ref[...] = solution
     res_ref[...] = residual
     for relay in relays:
         relay.finish_sends()
-    for k in range(ITERS):
+    for k in range(ITERS - 1):
         finish_put(k)
         finish_answer(k)
 
 
 def solve_cg(tile, targets_t, wide_factor, zed, inverse, proj, image, squares, n, width):
     rhs_count, row_count = targets_t.shape
-    owners = min(n, rhs_count)
+    owners = min(n // 2, rhs_count)
     per = rhs_count // owners
     order = wide_factor.shape[1]
     rows = -(-(order // LANES + 3) // 8) * 8
@@ -776,18 +863,20 @@
         out_specs=[vmem] * 2,
         scratch_shapes=[
             pltpu.VMEM((ITERS - 1, n, rhs_count, row_count), f32),
-            pltpu.VMEM((ITERS, rhs_count, rows, LANES), f32),
-            pltpu.VMEM((ITERS, n - 1, per, rows, LANES), f32),
-            pltpu.VMEM((ITERS, rhs_count, rows, LANES), f32),
+            pltpu.VMEM((ITERS - 1, rhs_count, rows, LANES), f32),
+            pltpu.VMEM((ITERS - 1, n - 1, per, rows, LANES), f32),
+            pltpu.VMEM((ITERS - 1, rhs_count, rows, LANES), f32),
             pltpu.VMEM((per, order), f32),
             pltpu.VMEM((per, LANES), f32),
             pltpu.VMEM((per, LANES), f32),
             pltpu.VMEM((rhs_count, LANES), f32),
+            pltpu.VMEM((n, 8, LANES), f32),
             pltpu.SemaphoreType.DMA((ITERS - 1,)),
             pltpu.SemaphoreType.DMA((ITERS - 1, n // 2)),
             pltpu.SemaphoreType.DMA((ITERS - 1,)),
         ]
-        + [pltpu.SemaphoreType.DMA((ITERS,))] * 4,
+        + [pltpu.SemaphoreType.DMA((ITERS - 1,))] * 4
+        + [pltpu.SemaphoreType.DMA] * 2,
         compiler_params=pltpu.CompilerParams(
             collective_id=2, has_side_effects=True, vmem_limit_bytes=60 * 2**20
         ),
@@ -795,19 +884,35 @@
     )(tile, targets_t, wide_factor, zed, inverse, proj, image, squares)
 
 
+def finish_kernel(wide_ref, solution_ref, residual_ref, factor_ref, solution_out, residual_out):
+    factor_ref[...] = wide_ref[...].astype(jnp.bfloat16)
+    solution_out[...] = solution_ref[...]
+    residual_out[...] = residual_ref[...]
+
+
+def finish(wide, solution_t, residual_t):
+    vmem = pl.BlockSpec(memory_space=pltpu.VMEM)
+    flat = jax.ShapeDtypeStruct(solution_t.shape, jnp.float32)
+    return pl.pallas_call(
+        finish_kernel,
+        out_shape=[jax.ShapeDtypeStruct(wide.shape, jnp.bfloat16), flat, flat],
+        in_specs=[vmem] * 3,
+        out_specs=[vmem] * 3,
+        name="finish_outputs",
+    )(wide, solution_t, residual_t)
+
+
 def per_device(n, width, points, targets, pivots):
     targets_t = targets.T
-    all_points, all_targets = gather_all(points, targets_t, n, width)
-    picked = all_points.reshape(-1, points.shape[1])[pivots.reshape(-1)]
-    order = picked.shape[0]
-    inverse = chol_inverse(pivot_kernel, picked, order, "pivot_inverse")
-    factor, wide, tile, gram, proj, zed, image, squares = sweep(
+    all_points, picked = gather_all(points, pivots, n, width)
+    inverse, all_targets = pivot_inverse(picked, targets_t, n, width)
+    wide, tile, gram, proj, zed, image, squares = sweep(
         all_points, all_targets, picked, inverse, n, width
     )
-    gram_inverse = chol_inverse(gram_kernel, gram, order, "gram_inverse")
     solution_t, residual_t = solve_cg(
-        tile, targets_t, wide, zed, gram_inverse, proj, image, squares, n, width
+        tile, targets_t, wide, zed, gram_inverse(gram), proj, image, squares, n, width
     )
+    factor, solution_t, residual_t = finish(wide, solution_t, residual_t)
     return (factor, solution_t.T, residual_t.T)
 
 

time: 141 us -> 127 us (0.901)
  local copies, waits for them, and re-layouts: 7.02 us -> 0 us
  Pallas kernels: 133 us -> 126 us
    pallas_call x1, Pallas kernels: 49.9 us -> 40.2 us  [solve_cg(): pl.pallas_call(functools.partial(cg_kernel, n, width, owners), out_shape=...]
    pallas_call x2 -> x3, Pallas kernels: 34.5 us -> 39 us  [the longest x1 20.1 us: pivot_inverse(): pl.pallas_call(functools.partial(pivot_kernel, n, width), out_shape=[jax....]
    unnamed x6 -> x0, local copies, waits for them, and re-layouts: 3.99 us -> none
    gather x1 -> x0, local copies, waits for them, and re-layouts: 3.03 us -> none  [per_device(): picked = all_points.reshape(-1, points.shape[1])[pivots.reshape(-1)]]
    pallas_call x1, Pallas kernels: 21.2 us -> 19.3 us  [gather_all(): pl.pallas_call(functools.partial(gather_kernel, n, width), out_shape=[jax...]
where the time goes in v3:
time: 127 us
  Pallas kernels  126 us (99%)
    pallas_call x1, Pallas kernels, solve_cg(): pl.pallas_call(functools.partial(cg_kernel, n, width, owners), out_shape=...  40.2 us
    pallas_call x1, Pallas kernels, sweep(): pl.pallas_call(functools.partial(sweep_kernel, n, width), out_shape=[jax....  27.5 us
    pallas_call x1, Pallas kernels, pivot_inverse(): pl.pallas_call(functools.partial(pivot_kernel, n, width), out_shape=[jax....  20.1 us
    pallas_call x1, Pallas kernels, gather_all(): pl.pallas_call(functools.partial(gather_kernel, n, width), out_shape=[jax...  19.3 us
    pallas_call x1, Pallas kernels, gram_inverse(): pl.pallas_call(gram_kernel, out_shape=jax.ShapeDtypeStruct(gram.shape, jn...  17.2 us

profile of v3, /device:TPU:0, one launch (start us, length us, event | category | flops | bytes accessed | tf_op | source)
XLA Modules:
  0.0 126.7 jit_solution(13599611409488600780)
XLA Ops:
  0.6 19.3 %gather_points.1 = (bf16[32,128,128]{2,1,0:T(8,128)(2,1)}, f32[512,128]{1,0:T(8,128)}) custom-call(bf16[128,128]{1,0:T(8,128)(2,1)} %points_ref.1, s32[2,256]{1,0:T(2,128)} %pivots_ref.1), custom_call_target="tpu_custom_call" | custom-call | tf_op jit(solution)/shard_map/gather_points/pallas_call | solution.py:425
  19.9 20.1 %pivot_inverse.1 = (f32[512,512]{1,0:T(8,128)}, f32[32,32,128]{2,1,0:T(8,128)}) custom-call(f32[512,128]{1,0:T(8,128)} %get-tuple-element.20.picked_ref, f32[32,128]{1,0:T(8,128)} %bitcast.9), custom_call_target="tpu_custom_call" | custom-call | tf_op jit(solution)/shard_map/pivot_inverse/pallas_call | solution.py:211
  40.1 27.5 %sweep_points.1 = (f32[128,512]{1,0:T(8,128)}, f32[16,2,128,128]{3,2,1,0:T(8,128)}, f32[512,512]{1,0:T(8,128)}, f32[32,512]{1,0:T(8,128)}, f32[128,512]{1,0:T(8,...) custom-call(bf16[16,2,128,128]{3,2,1,0:T(8,128)(2,1)} %bitcast.7, f32[16,2,32,128]{3,2,1,0:T(8,128)} %bitcast.8, ...), custom_call_target="tpu_custom_call" | custom-call | tf_op jit(solution)/shard_map/sweep_points/pallas_call | solution.py:577
  67.6 17.2 %gram_inverse.1.inverse_ref = f32[512,512]{1,0:T(8,128)} custom-call(f32[512,512]{1,0:T(8,128)} %get-tuple-element.26.gram_ref), custom_call_target="tpu_custom_call" | custom-call | tf_op jit(solution)/shard_map/gram_inverse/pallas_call | solution.py:237
  84.8 40.2 %conjugate_gradients.1 = (f32[32,128]{1,0:T(8,128)}, f32[32,128]{1,0:T(8,128)}) custom-call(f32[32,128,128]{2,1,0:T(8,128)} %bitcast.6, f32[32,128]{1,0:T(8,128)} %bitcast.10, f32[128,512]{1,0:T(8,128)} %get-tuple-element.23.wide_ref, f32[128,512]{1,0:T(8,128)} %get-tuple-element.25.zed_ref, f32[512,512]{1,0:T(8,128)} %gram_inverse.1.inverse_ref, ...), custom_call_target="tpu_custom_call" | custom-call | tf_op jit(solution)/shard_map/conjugate_gradients/pallas_call | solution.py:859
  125.0 1.6 %finish_outputs.1 = (bf16[128,512]{1,0:T(8,128)(2,1)}, f32[32,128]{1,0:T(8,128)}, f32[32,128]{1,0:T(8,128)}) custom-call(f32[128,512]{1,0:T(8,128)} %get-tuple-element.23.wide_ref, f32[32,128]{1,0:T(8,128)} %get-tuple-element.30.solution_ref, f32[32,128]{1,0:T(8,128)} %get-tuple-element.31.residual_ref), custom_call_target="tpu_custom_call" | custom-call | tf_op jit(solution)/shard_map/finish_outputs/pallas_call | solution.py:896

commit v4 on v3

--- a/solution.py
+++ b/solution.py
@@ -28,6 +28,33 @@
     )
 
 
+def pieces(values):
+    high = values.astype(jnp.bfloat16)
+    rest = values - high.astype(jnp.float32)
+    middle = rest.astype(jnp.bfloat16)
+    low = (rest - middle.astype(jnp.float32)).astype(jnp.bfloat16)
+    return high, middle, low
+
+
+def split_dot(stacked, refs, side):
+    step = stacked.shape[0] // 3
+    parts = [
+        lax.dot_general(
+            stacked[: (3 - k) * step],
+            refs[k],
+            (((1,), (side,)), ((), ())),
+            preferred_element_type=jnp.float32,
+        )
+        for k in range(3)
+    ]
+    total = parts[0][2 * step :] + parts[1][step : 2 * step] + parts[2]
+    return parts[0][:step] + (parts[0][step : 2 * step] + parts[1][:step] + total)
+
+
+def stack(values):
+    return jnp.concatenate(pieces(values), axis=0)
+
+
 def column_norms(point_rows):
     wide_rows = point_rows.astype(jnp.float32)
     return jnp.sum(wide_rows * wide_rows, axis=1, keepdims=True)
@@ -64,6 +91,7 @@
         end = start + group
         whole = []
         ahead = columns(rows[start], 8 * start)
+        pivot = full_of(ahead[0][0:1])
         for p in range(start, end):
             base = 8 * p
             inside = (lane >= base) & (lane < base + 8)
@@ -77,15 +105,21 @@
                 ahead = columns(rows[p + 1], base + 8)
                 following = jnp.where(inside, 0.0, rows[p + 1])
             for j in range(8):
-                pivot = full_of(cols[j][j : j + 1])
                 recip = 1.0 / pivot
                 pivots = jnp.where(sub == j, pivot, pivots)
-                below = jnp.where(sub > j, cols[j] * recip, 0.0)
+                coef = {c: full_of(cols[c][j : j + 1]) for c in range(j + 1, 8)}
+                if j < 7:
+                    square = full_of(cols[j][j + 1 : j + 2]) * coef[j + 1]
+                    pivot = full_of(cols[j + 1][j + 1 : j + 2]) - square * recip
+                elif more:
+                    corner = full_of(own[7][0:1])
+                    pivot = full_of(ahead[0][0:1]) - corner * corner * recip
+                scaled = cols[j] * recip
+                below = jnp.where(sub > j, scaled, 0.0)
                 spread_row = full_of(forward[j : j + 1])
                 forward = forward - below * spread_row
-                coef = {c: full_of(cols[c][j : j + 1]) for c in range(j + 1, 8)}
                 for c in range(j + 1, 8):
-                    cols[c] = cols[c] - below * coef[c]
+                    cols[c] = cols[c] - scaled * coef[c]
                 if more:
                     multiplier = own[j] * recip
                     for c in range(j + 1, 8):
@@ -113,56 +147,41 @@
                 rows[v] = new
         if end < count:
             side = jnp.concatenate(whole, axis=0)
-            both = lax.dot_general(
-                side,
-                side,
-                (((0,), (0,)), ((), ())),
-                precision=highest,
-                preferred_element_type=jnp.float32,
-            )
+            both = lax.dot_general(side, side, (((0,), (0,)), ((), ())), precision=highest, preferred_element_type=jnp.float32)
             inside = (lane >= 8 * start) & (lane < 8 * end)
             for v in range(end, count):
                 rows[v] = jnp.where(inside, 0.0, rows[v]) - both[8 * v : 8 * v + 8]
     return done
-
 
 def invert_lower(work, out_ref, beside=None):
     order = work.shape[0]
     blocks = order // LANES
     row_at = lax.broadcasted_iota(jnp.int32, (LANES, LANES), 0)
     col_at = lax.broadcasted_iota(jnp.int32, (LANES, LANES), 1)
-    lane_at = lax.broadcasted_iota(jnp.int32, (LANES, order), 1)
 
     def one_block(j, carry):
         at = pl.multiple_of(j * LANES, LANES)
-        here_rows = pl.ds(at, LANES)
         inverse = jnp.concatenate(
             lower_inverse_rows(
                 [work[pl.ds(at + 8 * v, 8), pl.ds(at, LANES)] for v in range(LANES // 8)]
             ),
             axis=0,
         )
-        work[here_rows, pl.ds(at, LANES)] = jnp.where(row_at == col_at, 1.0, 0.0)
-        side = jnp.dot(
-            inverse, work[here_rows, :], precision=highest, preferred_element_type=jnp.float32
-        )
-        out_ref[here_rows, :] = jnp.where(lane_at < at + LANES, side, 0.0)
-        work[here_rows, :] = side
-
-        def below(i, inner):
-            to = pl.multiple_of(i * LANES, LANES)
-            rows = work[pl.ds(to, LANES), :]
-            rows = jnp.where((lane_at >= at) & (lane_at < at + LANES), 0.0, rows)
-            work[pl.ds(to, LANES), :] = rows - lax.dot_general(
-                work[here_rows, pl.ds(to, LANES)],
-                side,
-                (((0,), (0,)), ((), ())),
-                precision=highest,
-                preferred_element_type=jnp.float32,
-            )
-            return inner
-
-        lax.fori_loop(j + 1, blocks, below, 0)
+        work[pl.ds(at, LANES), pl.ds(at, LANES)] = jnp.where(row_at == col_at, 1.0, 0.0)
+
+        def combine(k):
+            low, high = k * LANES, (k + 1) * LANES
+            side = jnp.dot(inverse, work[low:high, :], precision=highest, preferred_element_type=jnp.float32)
+            out_ref[low:high, :high] = side[:, :high]
+            if high < order:
+                out_ref[low:high, high:] = jnp.zeros((LANES, order - high), jnp.float32)
+                change = lax.dot_general(side[:, high:], side, (((0,), (0,)), ((), ())), precision=highest, preferred_element_type=jnp.float32)
+                if low: work[high:, :low] -= change[:, :low]
+                work[high:, low:high] = -change[:, low:high]
+                work[high:, high:] -= change[:, high:]
+
+        for k in range(blocks):
+            pl.when(j == k)(functools.partial(combine, k))
         if beside is not None:
             beside(j)
         return carry
@@ -227,19 +246,21 @@
     )(picked, targets_t)
 
 
-def gram_kernel(gram_ref, out_ref, work):
+def gram_kernel(gram_ref, split_ref, work, out_ref):
     work[...] = shifted(gram_ref[...], noise_level)
     invert_lower(work, out_ref)
+    for k, piece in enumerate(pieces(out_ref[...])):
+        split_ref[k] = piece
 
 
 def gram_inverse(gram):
     vmem = pl.BlockSpec(memory_space=pltpu.VMEM)
     return pl.pallas_call(
         gram_kernel,
-        out_shape=jax.ShapeDtypeStruct(gram.shape, jnp.float32),
+        out_shape=jax.ShapeDtypeStruct((3,) + gram.shape, jnp.bfloat16),
         in_specs=[vmem],
         out_specs=vmem,
-        scratch_shapes=[pltpu.VMEM(gram.shape, jnp.float32)],
+        scratch_shapes=[pltpu.VMEM(gram.shape, jnp.float32)] * 2,
         name="gram_inverse",
     )(gram)
 
@@ -459,6 +480,7 @@
     right_part,
     left_got,
     right_got,
+    crossed,
     send_sem,
     recv_sem,
 ):
@@ -476,29 +498,29 @@
     own = points_ref[pair, core]
     beside = points_ref[pair, other]
     own_column, beside_column = column_norms(own), column_norms(beside)
-    own_cross = kernel_block(own, own_column, picked, row_norms(picked))
-    wide = jnp.concatenate(
-        [
-            dot_t(own_cross[:, :half], inverse_ref[:half, :half]),
-            dot_t(own_cross, inverse_ref[half:, :]),
-        ],
-        axis=1,
-    )
-    wide_ref[...] = wide
     own_targets = targets_ref[pair, core]
     image_ref[...] = noise_level * own_targets
     square_ref[...] = jnp.zeros_like(square_ref)
     for ref in (left_part, right_part):
         ref[...] = jnp.zeros_like(ref)
 
+    steps = n // 2 // chunk
+
+    def cross_of(i):
+        at = i * chunk
+        near = jnp.concatenate([points_ref[at + t, core] for t in range(chunk)], axis=0)
+        return kernel_block(picked, picked_column, near, row_norms(near))
+
+    crossed[...] = cross_of(0)
+
     def step(i, carry):
         at = i * chunk
+        cross = crossed[...]
         near = jnp.concatenate([points_ref[at + t, core] for t in range(chunk)], axis=0)
         far = jnp.concatenate([points_ref[at + t, other] for t in range(chunk)], axis=0)
         near_targets = jnp.concatenate([targets_ref[at + t, core] for t in range(chunk)], axis=1)
         far_targets = jnp.concatenate([targets_ref[at + t, other] for t in range(chunk)], axis=1)
         near_row, far_row = row_norms(near), row_norms(far)
-        cross = kernel_block(picked, picked_column, near, near_row)
         own_near = kernel_block(own, own_column, near, near_row)
         own_far = kernel_block(own, own_column, far, far_row)
         beside_near = kernel_block(beside, beside_column, near, near_row)
@@ -519,16 +541,31 @@
             precision=highest,
             preferred_element_type=jnp.float32,
         )
+        crossed[...] = cross_of(jnp.minimum(i + 1, steps - 1))
         extra = [own_near, beside_near, near_targets]
         left_part[...] += dot_t(jnp.concatenate([top] + extra, axis=0), top)
         right_part[...] += dot_t(jnp.concatenate([top, low] + extra, axis=0), low)
-        image_ref[...] += dot_t(near_targets, own_near) + dot_t(far_targets, own_far)
+        image_ref[...] += split_dot(
+            stack(jnp.concatenate([near_targets, far_targets], axis=1)),
+            pieces(jnp.concatenate([own_near, own_far], axis=1)),
+            1,
+        )
         squares = near_targets * near_targets + far_targets * far_targets
         for t in range(chunk):
             square_ref[...] += squares[:, t * size : (t + 1) * size]
+
+        @pl.when(i == lax.div(pair, chunk))
+        def _():
+            for t in range(chunk):
+
+                @pl.when(lax.rem(pair, chunk) == t)
+                def _(t=t):
+                    for rows, value in ((slice(0, half), top), (slice(half, order), low)):
+                        wide_ref[:, rows] = value[:, t * size : (t + 1) * size].T
+
         return carry
 
-    lax.fori_loop(0, n // 2 // chunk, step, 0)
+    lax.fori_loop(0, steps, step, 0)
     pl.semaphore_wait(barrier, 1)
     size = own.shape[0]
     sides = [(left_part, left_got, half, 0), (right_part, right_got, order, half)]
@@ -590,7 +627,9 @@
         ],
         in_specs=[vmem] * 4,
         out_specs=[vmem] * 7,
-        scratch_shapes=partial * 2 + [pltpu.SemaphoreType.DMA((4,))] * 2,
+        scratch_shapes=partial * 2
+        + [pltpu.VMEM((order, min(4, n // 2) * rows), f32)]
+        + [pltpu.SemaphoreType.DMA((4,))] * 2,
         compiler_params=pltpu.CompilerParams(
             collective_id=1, has_side_effects=True, vmem_limit_bytes=60 * 2**20
         ),
@@ -627,6 +666,9 @@
     kept_rz,
     all_rz,
     ends,
+    narrow,
+    wide_split,
+    zed_split,
     dir_send,
     dir_recv,
     dir_pair,
@@ -723,24 +765,31 @@
         only_owners(body)
 
     def solve(proj):
-        half = dot_t(proj, inverse_ref[...])
-        coef = jnp.dot(
-            half, inverse_ref[...], precision=highest, preferred_element_type=jnp.float32
-        )
+        def stacked(values):
+            if values.shape[0] % 16 == 0:
+                return stack(values)
+            for t, piece in enumerate(pieces(values)):
+                narrow[8 * t : 8 * t + values.shape[0], :] = piece.astype(jnp.float32)
+            return narrow[...].astype(jnp.bfloat16)
+
+        count = proj.shape[0]
+        half = split_dot(stacked(proj), inverse_ref, 1)[:count]
+        coef = split_dot(stacked(half), inverse_ref, 0)[:count]
         return coef, wide_sum(half * half)
 
     def split(row):
         return [row[:, q * LANES : (q + 1) * LANES] for q in range(lanes)]
 
     def project(rows):
-        return jnp.dot(rows, wide_ref[...], precision=highest, preferred_element_type=jnp.float32)
+        return split_dot(stack(rows), wide_split, 0)
 
     def joined(packed):
         return jnp.concatenate([packed[:, q, :] for q in range(lanes)], axis=1)
 
     def preconditioned(coef, residual, applied):
-        direction = (residual - dot_t(coef, wide_ref[...])) * (1.0 / noise_level)
-        image = (applied - dot_t(coef, zed_ref[...])) * (1.0 / noise_level)
+        stacked = stack(coef)
+        direction = (residual - split_dot(stacked, wide_split, 1)) * (1.0 / noise_level)
+        image = (applied - split_dot(stacked, zed_split, 1)) * (1.0 / noise_level)
         return direction, image
 
     def multiplied(k, image):
@@ -749,6 +798,10 @@
 
         return lax.fori_loop(0, n, one, noise_level * image, unroll=4)
 
+    narrow[...] = jnp.zeros_like(narrow)
+    for split_ref, ref in ((wide_split, wide_ref), (zed_split, zed_ref)):
+        for t, piece in enumerate(pieces(ref[...])):
+            split_ref[t] = piece
     residual = rhs_ref[...]
     applied = image_ref[...]
     solution = jnp.zeros_like(residual)
@@ -871,6 +924,9 @@
             pltpu.VMEM((per, LANES), f32),
             pltpu.VMEM((rhs_count, LANES), f32),
             pltpu.VMEM((n, 8, LANES), f32),
+            pltpu.VMEM((24, order), f32),
+            pltpu.VMEM((3,) + wide_factor.shape, jnp.bfloat16),
+            pltpu.VMEM((3,) + wide_factor.shape, jnp.bfloat16),
             pltpu.SemaphoreType.DMA((ITERS - 1,)),
             pltpu.SemaphoreType.DMA((ITERS - 1, n // 2)),
             pltpu.SemaphoreType.DMA((ITERS - 1,)),

time: 127 us -> 123 us (0.969)
  Pallas kernels: 126 us -> 122 us
    pallas_call x1, Pallas kernels: 40.2 us -> 38.6 us  [solve_cg(): pl.pallas_call(functools.partial(cg_kernel, n, width, owners), out_shape=...]
where the time goes in v4:
time: 123 us
  Pallas kernels  122 us (99%)
    pallas_call x1, Pallas kernels, solve_cg(): pl.pallas_call(functools.partial(cg_kernel, n, width, owners), out_shape=...  38.6 us
    pallas_call x1, Pallas kernels, sweep(): pl.pallas_call(functools.partial(sweep_kernel, n, width), out_shape=[jax....  27.2 us
    pallas_call x1, Pallas kernels, gather_all(): pl.pallas_call(functools.partial(gather_kernel, n, width), out_shape=[jax...  19.3 us
    pallas_call x1, Pallas kernels, pivot_inverse(): pl.pallas_call(functools.partial(pivot_kernel, n, width), out_shape=[jax....  19.1 us
    pallas_call x1, Pallas kernels, gram_inverse(): pl.pallas_call(gram_kernel, out_shape=jax.ShapeDtypeStruct((3,) + gram.sh...  16.3 us

profile of v4, /device:TPU:0, one launch (start us, length us, event | category | flops | bytes accessed | tf_op | source)
XLA Modules:
  0.0 122.9 jit_solution(14002756785916730589)
XLA Ops:
  0.6 19.3 %gather_points.1 = (bf16[32,128,128]{2,1,0:T(8,128)(2,1)}, f32[512,128]{1,0:T(8,128)}) custom-call(bf16[128,128]{1,0:T(8,128)(2,1)} %points_ref.1, s32[2,256]{1,0:T(2,128)} %pivots_ref.1), custom_call_target="tpu_custom_call" | custom-call | tf_op jit(solution)/shard_map/gather_points/pallas_call | solution.py:446
  19.9 19.1 %pivot_inverse.1 = (f32[512,512]{1,0:T(8,128)}, f32[32,32,128]{2,1,0:T(8,128)}) custom-call(f32[512,128]{1,0:T(8,128)} %get-tuple-element.20.picked_ref, f32[32,128]{1,0:T(8,128)} %bitcast.9), custom_call_target="tpu_custom_call" | custom-call | tf_op jit(solution)/shard_map/pivot_inverse/pallas_call | solution.py:230
  39.0 27.2 %sweep_points.1 = (f32[128,512]{1,0:T(8,128)}, f32[16,2,128,128]{3,2,1,0:T(8,128)}, f32[512,512]{1,0:T(8,128)}, f32[32,512]{1,0:T(8,128)}, f32[128,512]{1,0:T(8,...) custom-call(bf16[16,2,128,128]{3,2,1,0:T(8,128)(2,1)} %bitcast.7, f32[16,2,32,128]{3,2,1,0:T(8,128)} %bitcast.8, ...), custom_call_target="tpu_custom_call" | custom-call | tf_op jit(solution)/shard_map/sweep_points/pallas_call | solution.py:614
  66.3 16.3 %gram_inverse.1.inverse_ref = bf16[3,512,512]{2,1,0:T(8,128)(2,1)} custom-call(f32[512,512]{1,0:T(8,128)} %get-tuple-element.26.gram_ref), custom_call_target="tpu_custom_call" | custom-call | tf_op jit(solution)/shard_map/gram_inverse/pallas_call | solution.py:258
  82.6 38.6 %conjugate_gradients.1 = (f32[32,128]{1,0:T(8,128)}, f32[32,128]{1,0:T(8,128)}) custom-call(f32[32,128,128]{2,1,0:T(8,128)} %bitcast.6, f32[32,128]{1,0:T(8,128)} %bitcast.10, f32[128,512]{1,0:T(8,128)} %get-tuple-element.23.wide_ref, f32[128,512]{1,0:T(8,128)} %get-tuple-element.25.zed_ref, bf16[3,512,512]{2,1,0:T(8,128)(2,1)} %gram_inverse.1.inverse_ref, ...), custom_call_target="tpu_custom_call" | custom-call | tf_op jit(solution)/shard_map/conjugate_gradients/pallas_call | solution.py:912
  121.2 1.6 %finish_outputs.1 = (bf16[128,512]{1,0:T(8,128)(2,1)}, f32[32,128]{1,0:T(8,128)}, f32[32,128]{1,0:T(8,128)}) custom-call(f32[128,512]{1,0:T(8,128)} %get-tuple-element.23.wide_ref, f32[32,128]{1,0:T(8,128)} %get-tuple-element.30.solution_ref, f32[32,128]{1,0:T(8,128)} %get-tuple-element.31.residual_ref), custom_call_target="tpu_custom_call" | custom-call | tf_op jit(solution)/shard_map/finish_outputs/pallas_call | solution.py:952

commit v5 on v4

--- a/solution.py
+++ b/solution.py
@@ -199,18 +199,18 @@
     n, width, picked_ref, targets_ref, out_ref, all_targets, work, send_sem, recv_sems, pair_sem
 ):
     me = here(width)
-    hello(n, width, me)
     all_targets[me] = targets_ref[...]
     relay = Relay(
         n, width, me, all_targets, all_targets.at[me], send_sem, recv_sems, pair_sem
     )
+    relay.hello()
     picked = picked_ref[...].astype(jnp.bfloat16)
     work[...] = shifted(
         kernel_block(picked, column_norms(picked), picked, row_norms(picked)), jitter_level
     )
 
     def begin():
-        all_here(n)
+        relay.all_here()
         relay.start()
 
     def beside(j):
@@ -239,7 +239,7 @@
             pltpu.VMEM((order, order), f32),
             pltpu.SemaphoreType.DMA,
             pltpu.SemaphoreType.DMA((n // 2,)),
-            pltpu.SemaphoreType.DMA,
+            pltpu.SemaphoreType.DMA((width,)),
         ],
         compiler_params=pltpu.CompilerParams(collective_id=3, has_side_effects=True),
         name="pivot_inverse",
@@ -321,12 +321,34 @@
 
 
 class Relay:
-    def __init__(self, n, width, me, blocks, own, send_sem, recv_sems, pair_sem):
+    def __init__(self, n, width, me, blocks, own, send_sem, recv_sems, pair_sems):
         self.n, self.width, self.me = n, width, me
         self.blocks, self.own = blocks, own
-        self.send_sem, self.recv_sems, self.pair_sem = send_sem, recv_sems, pair_sem
+        self.send_sem, self.recv_sems, self.pair_sems = send_sem, recv_sems, pair_sems
         self.plane = 2 * width
         self.lines = n // self.plane
+
+    def hello(self):
+        barrier = pltpu.get_barrier_semaphore()
+
+        def signal(peer):
+            pl.semaphore_signal(
+                barrier, inc=1, device_id=coords(peer, self.width), device_id_type=MESH
+            )
+
+        def along(i, carry):
+            signal(lax.rem(self.me + self.plane * i, self.n))
+            return carry
+
+        lax.fori_loop(1, self.lines, along, 0)
+        for q in range(2, self.plane, 2):
+            signal(flip(self.me, q))
+        signal(flip(self.me, 1))
+
+    def all_here(self):
+        pl.semaphore_wait(
+            pltpu.get_barrier_semaphore(), self.lines - 1 + self.plane // 2
+        )
 
     def send(self, src_ref, source, peer, recv_sem):
         pltpu.make_async_remote_copy(
@@ -342,7 +364,7 @@
         for q in range(2, self.plane, 2):
             sem = self.recv_sems.at[self.lines * (q // 2) + i]
             self.send(src_ref, source, flip(self.me, q), sem)
-        self.send(src_ref, source, flip(self.me, 1), self.pair_sem)
+        self.send(src_ref, source, flip(self.me, 1), self.pair_sems.at[0])
 
     def start(self):
         def along(i, carry):
@@ -369,13 +391,14 @@
                 source = lax.rem(flip(self.me, q) - self.plane * i + self.n, self.n)
                 ref = self.blocks.at[source]
                 drain(ref, self.recv_sems.at[self.lines * (q // 2) + i])
-                self.send(ref, source, flip(self.me, 1), self.pair_sem)
+                self.send(ref, source, flip(self.me, 1), self.pair_sems.at[q // 2])
                 return carry
 
             lax.fori_loop(0, self.lines, one, 0)
 
-    def finish(self):
-        drain(self.blocks.at[pl.ds(0, self.n // 2)], self.pair_sem)
+    def finish(self, *offsets):
+        for q in offsets or range(0, self.plane, 2):
+            drain(self.blocks.at[pl.ds(0, self.lines)], self.pair_sems.at[q // 2])
 
     def finish_sends(self):
         drain(self.blocks.at[pl.ds(0, self.n - 1)], self.send_sem)
@@ -394,10 +417,10 @@
     own_sem,
 ):
     me = here(width)
-    hello(n, width, me)
+    relay = Relay(n, width, me, all_points, points_ref, send_sem, recv_sems, pair_sem)
+    relay.hello()
     keep = pltpu.make_async_copy(points_ref, all_points.at[me], own_sem)
     keep.start()
-    relay = Relay(n, width, me, all_points, points_ref, send_sem, recv_sems, pair_sem)
     rows = points_ref.shape[0]
     order = picked_ref.shape[0]
     pivots = pivots_ref[...].astype(jnp.float32)
@@ -407,7 +430,7 @@
     row_at = lax.broadcasted_iota(jnp.int32, (order, rows), 1).astype(jnp.float32)
     together = min(4, relay.lines)
     picked_ref[...] = jnp.zeros_like(picked_ref)
-    all_here(n)
+    relay.all_here()
     relay.start()
 
     def pick(group):
@@ -434,8 +457,8 @@
     for q in range(2, relay.plane, 2):
         relay.relay_plane(q)
         pick(low(q))
-    relay.finish()
     for q in range(0, relay.plane, 2):
+        relay.finish(q)
         pick(low(q + 1))
     relay.finish_sends()
 
@@ -454,7 +477,7 @@
         scratch_shapes=[
             pltpu.SemaphoreType.DMA,
             pltpu.SemaphoreType.DMA((n // 2,)),
-            pltpu.SemaphoreType.DMA,
+            pltpu.SemaphoreType.DMA((width,)),
             pltpu.SemaphoreType.DMA,
         ],
         compiler_params=pltpu.CompilerParams(collective_id=0, has_side_effects=True),
@@ -929,7 +952,7 @@
             pltpu.VMEM((3,) + wide_factor.shape, jnp.bfloat16),
             pltpu.SemaphoreType.DMA((ITERS - 1,)),
             pltpu.SemaphoreType.DMA((ITERS - 1, n // 2)),
-            pltpu.SemaphoreType.DMA((ITERS - 1,)),
+            pltpu.SemaphoreType.DMA((ITERS - 1, width)),
         ]
         + [pltpu.SemaphoreType.DMA((ITERS - 1,))] * 4
         + [pltpu.SemaphoreType.DMA] * 2,

time: 123 us -> 122 us (level)
  no operation moved by 1% of the time
where the time goes in v5:
time: 122 us
  Pallas kernels  121 us (99%)
    pallas_call x1, Pallas kernels, solve_cg(): pl.pallas_call(functools.partial(cg_kernel, n, width, owners), out_shape=...  39.7 us
    pallas_call x1, Pallas kernels, sweep(): pl.pallas_call(functools.partial(sweep_kernel, n, width), out_shape=[jax....  27.1 us
    pallas_call x1, Pallas kernels, gather_all(): pl.pallas_call(functools.partial(gather_kernel, n, width), out_shape=[jax...  18.1 us
    pallas_call x1, Pallas kernels, pivot_inverse(): pl.pallas_call(functools.partial(pivot_kernel, n, width), out_shape=[jax....  18 us
    pallas_call x1, Pallas kernels, gram_inverse(): pl.pallas_call(gram_kernel, out_shape=jax.ShapeDtypeStruct((3,) + gram.sh...  16.3 us

profile of v5, /device:TPU:0, one launch (start us, length us, event | category | flops | bytes accessed | tf_op | source)
XLA Modules:
  0.0 121.6 jit_solution(2275758000892510851)
XLA Ops:
  0.6 18.1 %gather_points.1 = (bf16[32,128,128]{2,1,0:T(8,128)(2,1)}, f32[512,128]{1,0:T(8,128)}) custom-call(bf16[128,128]{1,0:T(8,128)(2,1)} %points_ref.1, s32[2,256]{1,0:T(2,128)} %pivots_ref.1), custom_call_target="tpu_custom_call" | custom-call | tf_op jit(solution)/shard_map/gather_points/pallas_call | solution.py:469
  18.8 18.0 %pivot_inverse.1 = (f32[512,512]{1,0:T(8,128)}, f32[32,32,128]{2,1,0:T(8,128)}) custom-call(f32[512,128]{1,0:T(8,128)} %get-tuple-element.20.picked_ref, f32[32,128]{1,0:T(8,128)} %bitcast.9), custom_call_target="tpu_custom_call" | custom-call | tf_op jit(solution)/shard_map/pivot_inverse/pallas_call | solution.py:230
  36.7 27.1 %sweep_points.1 = (f32[128,512]{1,0:T(8,128)}, f32[16,2,128,128]{3,2,1,0:T(8,128)}, f32[512,512]{1,0:T(8,128)}, f32[32,512]{1,0:T(8,128)}, f32[128,512]{1,0:T(8,...) custom-call(bf16[16,2,128,128]{3,2,1,0:T(8,128)(2,1)} %bitcast.7, f32[16,2,32,128]{3,2,1,0:T(8,128)} %bitcast.8, ...), custom_call_target="tpu_custom_call" | custom-call | tf_op jit(solution)/shard_map/sweep_points/pallas_call | solution.py:637
  63.9 16.3 %gram_inverse.1.inverse_ref = bf16[3,512,512]{2,1,0:T(8,128)(2,1)} custom-call(f32[512,512]{1,0:T(8,128)} %get-tuple-element.26.gram_ref), custom_call_target="tpu_custom_call" | custom-call | tf_op jit(solution)/shard_map/gram_inverse/pallas_call | solution.py:258
  80.2 39.7 %conjugate_gradients.1 = (f32[32,128]{1,0:T(8,128)}, f32[32,128]{1,0:T(8,128)}) custom-call(f32[32,128,128]{2,1,0:T(8,128)} %bitcast.6, f32[32,128]{1,0:T(8,128)} %bitcast.10, f32[128,512]{1,0:T(8,128)} %get-tuple-element.23.wide_ref, f32[128,512]{1,0:T(8,128)} %get-tuple-element.25.zed_ref, bf16[3,512,512]{2,1,0:T(8,128)(2,1)} %gram_inverse.1.inverse_ref, ...), custom_call_target="tpu_custom_call" | custom-call | tf_op jit(solution)/shard_map/conjugate_gradients/pallas_call | solution.py:935
  119.9 1.6 %finish_outputs.1 = (bf16[128,512]{1,0:T(8,128)(2,1)}, f32[32,128]{1,0:T(8,128)}, f32[32,128]{1,0:T(8,128)}) custom-call(f32[128,512]{1,0:T(8,128)} %get-tuple-element.23.wide_ref, f32[32,128]{1,0:T(8,128)} %get-tuple-element.30.solution_ref, f32[32,128]{1,0:T(8,128)} %get-tuple-element.31.residual_ref), custom_call_target="tpu_custom_call" | custom-call | tf_op jit(solution)/shard_map/finish_outputs/pallas_call | solution.py:975

commit v6 on v5

--- a/solution.py
+++ b/solution.py
@@ -711,7 +711,18 @@
     rank = me - first_owner
     owning = (rank >= 0) & (rank < owners)
     own_rows = pl.ds(rank * per, per)
+    sent = pl.ds(0, lanes + 1)
     hello(n, width, me)
+
+    def packed_row(values):
+        lane_at = lax.broadcasted_iota(jnp.int32, values[0].shape, 1)
+        row = values[-1]
+        for s in range(len(values) - 1):
+            row = jnp.where(lane_at == s, values[s], row)
+        return row
+
+    def unpacked(row, s):
+        return jnp.broadcast_to(row[:, s : s + 1], row.shape)
 
     def only_owners(body):
         pl.when(owning)(body)
@@ -722,8 +733,7 @@
     def to_owners(k, proj, sums):
         for q in range(lanes):
             put[k, :, q, :] = proj[:, q * LANES : (q + 1) * LANES]
-        for s, value in enumerate(sums):
-            put[k, :, lanes + s, :] = value
+        put[k, :, lanes, :] = packed_row(sums)
 
         def push(i, carry):
             turn = lax.rem(me + i, owners)
@@ -732,8 +742,8 @@
             @pl.when(peer != me)
             def _():
                 pltpu.make_async_remote_copy(
-                    src_ref=put.at[k, pl.ds(turn * per, per)],
-                    dst_ref=got.at[k, lax.rem(me - peer + n, n) - 1],
+                    src_ref=put.at[k, pl.ds(turn * per, per), sent],
+                    dst_ref=got.at[k, lax.rem(me - peer + n, n) - 1, :, sent],
                     send_sem=put_send.at[k],
                     recv_sem=put_recv.at[k],
                     device_id=coords(peer, width),
@@ -754,12 +764,12 @@
             drain(ref, sem)
 
     def finish_put(k):
-        drain_others(put.at[k], put_send.at[k])
+        drain_others(put.at[k, :, sent], put_send.at[k])
 
     def collect(k):
-        drain(got.at[k], put_recv.at[k])
-        start = put[k, own_rows]
-        return lax.fori_loop(0, n - 1, lambda i, acc: acc + got[k, i], start)
+        drain(got.at[k, :, :, sent], put_recv.at[k])
+        start = put[k, own_rows, : lanes + 1]
+        return lax.fori_loop(0, n - 1, lambda i, acc: acc + got[k, i, :, : lanes + 1], start)
 
     def answer(k, rows):
         for s, value in enumerate(rows):
@@ -768,19 +778,19 @@
             n,
             width,
             me,
-            lambda peer, i: ans.at[k, own_rows],
-            lambda peer, i: ans.at[k, own_rows],
+            lambda peer, i: ans.at[k, own_rows, sent],
+            lambda peer, i: ans.at[k, own_rows, sent],
             ans_send.at[k],
             ans_recv.at[k],
         )
 
     def await_answer(k):
-        drain_others(ans.at[k], ans_recv.at[k])
+        drain_others(ans.at[k, :, sent], ans_recv.at[k])
 
     def finish_answer(k):
         def body():
             def one(i, carry):
-                drain(ans.at[k, pl.ds(0, per)], ans_send.at[k])
+                drain(ans.at[k, pl.ds(0, per), sent], ans_send.at[k])
                 return carry
 
             lax.fori_loop(1, n, one, 0)
@@ -844,8 +854,9 @@
 
     def later_answer(k):
         total = collect(k)
-        size = kept_rz[...] / total[:, lanes, :]
-        along, image_squares = total[:, lanes + 1, :], total[:, lanes + 2, :]
+        sums = total[:, lanes, :]
+        size = kept_rz[...] / unpacked(sums, 0)
+        along, image_squares = unpacked(sums, 1), unpacked(sums, 2)
         size_row = jnp.concatenate([size] * lanes, axis=1)
         proj = kept_proj[...] - size_row * joined(total)
         squares = kept_squares[...] - 2.0 * size * along + size * size * image_squares
@@ -854,7 +865,7 @@
         kept_proj[...] = proj
         kept_squares[...] = squares
         kept_rz[...] = rz
-        answer(k, split(coef) + [size, rz])
+        answer(k, split(coef) + [packed_row([size, rz])])
 
     def last_sums(values):
         ends[me, 0:1, 0:rhs_count] = dot_t(jnp.ones((8, row_count), jnp.float32), values)[0:1]
@@ -902,8 +913,8 @@
         relay.finish()
         twice = multiplied(k, image)
         await_answer(k)
-        size = ans[k, :, lanes, :]
-        rz = ans[k, :, lanes + 1, :]
+        scalars = ans[k, :, lanes, :]
+        size, rz = unpacked(scalars, 0), unpacked(scalars, 1)
         ratio = rz / all_rz[...]
         all_rz[...] = rz
         solution = solution + size * direction

time: 122 us -> 120 us (0.984)
  Pallas kernels: 121 us -> 119 us
    pallas_call x1, Pallas kernels: 39.7 us -> 37.6 us  [solve_cg(): pl.pallas_call(functools.partial(cg_kernel, n, width, owners), out_shape=...]
where the time goes in v6:
time: 120 us; the launch traced here: 119 us
  Pallas kernels  119 us (99%)
    pallas_call x1, Pallas kernels, solve_cg(): pl.pallas_call(functools.partial(cg_kernel, n, width, owners), out_shape=...  37.6 us
    pallas_call x1, Pallas kernels, sweep(): pl.pallas_call(functools.partial(sweep_kernel, n, width), out_shape=[jax....  27.1 us
    pallas_call x1, Pallas kernels, gather_all(): pl.pallas_call(functools.partial(gather_kernel, n, width), out_shape=[jax...  18.1 us
    pallas_call x1, Pallas kernels, pivot_inverse(): pl.pallas_call(functools.partial(pivot_kernel, n, width), out_shape=[jax....  18 us
    pallas_call x1, Pallas kernels, gram_inverse(): pl.pallas_call(gram_kernel, out_shape=jax.ShapeDtypeStruct((3,) + gram.sh...  16.3 us

profile of v6, /device:TPU:0, one launch (start us, length us, event | category | flops | bytes accessed | tf_op | source)
XLA Modules:
  0.0 119.4 jit_solution(15851278010845950936)
XLA Ops:
  0.6 18.1 %gather_points.1 = (bf16[32,128,128]{2,1,0:T(8,128)(2,1)}, f32[512,128]{1,0:T(8,128)}) custom-call(bf16[128,128]{1,0:T(8,128)(2,1)} %points_ref.1, s32[2,256]{1,0:T(2,128)} %pivots_ref.1), custom_call_target="tpu_custom_call" | custom-call | tf_op jit(solution)/shard_map/gather_points/pallas_call | solution.py:469
  18.8 18.0 %pivot_inverse.1 = (f32[512,512]{1,0:T(8,128)}, f32[32,32,128]{2,1,0:T(8,128)}) custom-call(f32[512,128]{1,0:T(8,128)} %get-tuple-element.20.picked_ref, f32[32,128]{1,0:T(8,128)} %bitcast.9), custom_call_target="tpu_custom_call" | custom-call | tf_op jit(solution)/shard_map/pivot_inverse/pallas_call | solution.py:230
  36.7 27.1 %sweep_points.1 = (f32[128,512]{1,0:T(8,128)}, f32[16,2,128,128]{3,2,1,0:T(8,128)}, f32[512,512]{1,0:T(8,128)}, f32[32,512]{1,0:T(8,128)}, f32[128,512]{1,0:T(8,...) custom-call(bf16[16,2,128,128]{3,2,1,0:T(8,128)(2,1)} %bitcast.7, f32[16,2,32,128]{3,2,1,0:T(8,128)} %bitcast.8, ...), custom_call_target="tpu_custom_call" | custom-call | tf_op jit(solution)/shard_map/sweep_points/pallas_call | solution.py:637
  63.9 16.3 %gram_inverse.1.inverse_ref = bf16[3,512,512]{2,1,0:T(8,128)(2,1)} custom-call(f32[512,512]{1,0:T(8,128)} %get-tuple-element.26.gram_ref), custom_call_target="tpu_custom_call" | custom-call | tf_op jit(solution)/shard_map/gram_inverse/pallas_call | solution.py:258
  80.2 37.6 %conjugate_gradients.1 = (f32[32,128]{1,0:T(8,128)}, f32[32,128]{1,0:T(8,128)}) custom-call(f32[32,128,128]{2,1,0:T(8,128)} %bitcast.6, f32[32,128]{1,0:T(8,128)} %bitcast.10, f32[128,512]{1,0:T(8,128)} %get-tuple-element.23.wide_ref, f32[128,512]{1,0:T(8,128)} %get-tuple-element.25.zed_ref, bf16[3,512,512]{2,1,0:T(8,128)(2,1)} %gram_inverse.1.inverse_ref, ...), custom_call_target="tpu_custom_call" | custom-call | tf_op jit(solution)/shard_map/conjugate_gradients/pallas_call | solution.py:946
  117.8 1.6 %finish_outputs.1 = (bf16[128,512]{1,0:T(8,128)(2,1)}, f32[32,128]{1,0:T(8,128)}, f32[32,128]{1,0:T(8,128)}) custom-call(f32[128,512]{1,0:T(8,128)} %get-tuple-element.23.wide_ref, f32[32,128]{1,0:T(8,128)} %get-tuple-element.30.solution_ref, f32[32,128]{1,0:T(8,128)} %get-tuple-element.31.residual_ref), custom_call_target="tpu_custom_call" | custom-call | tf_op jit(solution)/shard_map/finish_outputs/pallas_call | solution.py:986

commit v7 on v6

--- a/solution.py
+++ b/solution.py
@@ -825,11 +825,11 @@
         image = (applied - split_dot(stacked, zed_split, 1)) * (1.0 / noise_level)
         return direction, image
 
-    def multiplied(k, image):
-        def one(j, acc):
-            return acc + dot_t(dirs[k, j], tile_ref[j])
-
-        return lax.fori_loop(0, n, one, noise_level * image, unroll=4)
+    def multiplied(k, core, start):
+        def one(i, acc):
+            return acc + dot_t(dirs[k, 2 * i + core], tile_ref[2 * i + core])
+
+        return lax.fori_loop(0, n // 2, one, start, unroll=4)
 
     narrow[...] = jnp.zeros_like(narrow)
     for split_ref, ref in ((wide_split, wide_ref), (zed_split, zed_ref)):
@@ -910,8 +910,9 @@
         relay.relay_lines()
         only_owners(functools.partial(later_answer, k))
         relay.relay_plane()
+        twice = multiplied(k, lax.rem(me, 2), noise_level * image)
         relay.finish()
-        twice = multiplied(k, image)
+        twice = multiplied(k, 1 - lax.rem(me, 2), twice)
         await_answer(k)
         scalars = ans[k, :, lanes, :]
         size, rz = unpacked(scalars, 0), unpacked(scalars, 1)

time: 120 us -> 118 us (0.983)
  Pallas kernels: 119 us -> 117 us
    pallas_call x1, Pallas kernels: 37.6 us -> 36.3 us  [solve_cg(): pl.pallas_call(functools.partial(cg_kernel, n, width, owners), out_shape=...]
where the time goes in v7:
time: 118 us
  Pallas kernels  117 us (99%)
    pallas_call x1, Pallas kernels, solve_cg(): pl.pallas_call(functools.partial(cg_kernel, n, width, owners), out_shape=...  36.3 us
    pallas_call x1, Pallas kernels, sweep(): pl.pallas_call(functools.partial(sweep_kernel, n, width), out_shape=[jax....  27.1 us
    pallas_call x1, Pallas kernels, gather_all(): pl.pallas_call(functools.partial(gather_kernel, n, width), out_shape=[jax...  18.1 us
    pallas_call x1, Pallas kernels, pivot_inverse(): pl.pallas_call(functools.partial(pivot_kernel, n, width), out_shape=[jax....  18 us
    pallas_call x1, Pallas kernels, gram_inverse(): pl.pallas_call(gram_kernel, out_shape=jax.ShapeDtypeStruct((3,) + gram.sh...  16.3 us

profile of v7, /device:TPU:0, one launch (start us, length us, event | category | flops | bytes accessed | tf_op | source)
XLA Modules:
  0.0 118.1 jit_solution(12645059517630459951)
XLA Ops:
  0.6 18.1 %gather_points.1 = (bf16[32,128,128]{2,1,0:T(8,128)(2,1)}, f32[512,128]{1,0:T(8,128)}) custom-call(bf16[128,128]{1,0:T(8,128)(2,1)} %points_ref.1, s32[2,256]{1,0:T(2,128)} %pivots_ref.1), custom_call_target="tpu_custom_call" | custom-call | tf_op jit(solution)/shard_map/gather_points/pallas_call | solution.py:469
  18.8 18.0 %pivot_inverse.1 = (f32[512,512]{1,0:T(8,128)}, f32[32,32,128]{2,1,0:T(8,128)}) custom-call(f32[512,128]{1,0:T(8,128)} %get-tuple-element.20.picked_ref, f32[32,128]{1,0:T(8,128)} %bitcast.9), custom_call_target="tpu_custom_call" | custom-call | tf_op jit(solution)/shard_map/pivot_inverse/pallas_call | solution.py:230
  36.7 27.1 %sweep_points.1 = (f32[128,512]{1,0:T(8,128)}, f32[16,2,128,128]{3,2,1,0:T(8,128)}, f32[512,512]{1,0:T(8,128)}, f32[32,512]{1,0:T(8,128)}, f32[128,512]{1,0:T(8,...) custom-call(bf16[16,2,128,128]{3,2,1,0:T(8,128)(2,1)} %bitcast.7, f32[16,2,32,128]{3,2,1,0:T(8,128)} %bitcast.8, ...), custom_call_target="tpu_custom_call" | custom-call | tf_op jit(solution)/shard_map/sweep_points/pallas_call | solution.py:637
  63.9 16.3 %gram_inverse.1.inverse_ref = bf16[3,512,512]{2,1,0:T(8,128)(2,1)} custom-call(f32[512,512]{1,0:T(8,128)} %get-tuple-element.26.gram_ref), custom_call_target="tpu_custom_call" | custom-call | tf_op jit(solution)/shard_map/gram_inverse/pallas_call | solution.py:258
  80.2 36.3 %conjugate_gradients.1 = (f32[32,128]{1,0:T(8,128)}, f32[32,128]{1,0:T(8,128)}) custom-call(f32[32,128,128]{2,1,0:T(8,128)} %bitcast.6, f32[32,128]{1,0:T(8,128)} %bitcast.10, f32[128,512]{1,0:T(8,128)} %get-tuple-element.23.wide_ref, f32[128,512]{1,0:T(8,128)} %get-tuple-element.25.zed_ref, bf16[3,512,512]{2,1,0:T(8,128)(2,1)} %gram_inverse.1.inverse_ref, ...), custom_call_target="tpu_custom_call" | custom-call | tf_op jit(solution)/shard_map/conjugate_gradients/pallas_call | solution.py:947
  116.5 1.6 %finish_outputs.1 = (bf16[128,512]{1,0:T(8,128)(2,1)}, f32[32,128]{1,0:T(8,128)}, f32[32,128]{1,0:T(8,128)}) custom-call(f32[128,512]{1,0:T(8,128)} %get-tuple-element.23.wide_ref, f32[32,128]{1,0:T(8,128)} %get-tuple-element.30.solution_ref, f32[32,128]{1,0:T(8,128)} %get-tuple-element.31.residual_ref), custom_call_target="tpu_custom_call" | custom-call | tf_op jit(solution)/shard_map/finish_outputs/pallas_call | solution.py:987
